TPU v7x, 32 devices: a whole 2x2x4 slice. The times are simulated.
32 devices in a mesh: dp: 8 (over y, x, core), mp: 4 (over z).
Axes of the slice: x: 2, y: 2, z: 4, core: 2. Of those that a mesh axis runs over, the one named last changes fastest.
Arguments:
- inputs: float32 [16384, 1152], P('dp'), may hold values from -6 to 6
- cotangent: float32 [16384, 1152], P('dp'), may hold values from -6 to 6
- lengths: int32 [32, 3], P('dp'), may hold values from 0 to 512, as said below
- padding: int32 [32], P('dp'), may hold values from 0 to 127
- timesteps: int32 [32, 3], P('dp'), may hold values from 0 to 999
- classes: int32 [32, 3], P('dp'), may hold values from 0 to 999
- crop_head_mask: int32 [32, 3, 16], P('dp', None, 'mp'), may hold values 0 or 1
- channel_group_mask: int32 [32, 3, 16], P('dp', None, 'mp'), may hold values 0 or 1
- token_skip_flag: int32 [16384], P('dp'), may hold values 0 or 1
- time_weight: bfloat16 [256, 1152], P(None, 'mp'), may hold values from -0.375 to 0.375
- class_table: bfloat16 [1000, 1152], P(None, 'mp'), may hold values from -6 to 6
- ada_weight: bfloat16 [1152, 6, 1152], P('mp'), may hold values from -0.1875 to 0.1875
- ada_bias: float32 [6, 1152], replicated, may hold values from -4 to 4
- qkv_weight: bfloat16 [3, 1152, 1152], P(None, None, 'mp'), may hold values from -0.1875 to 0.1875
- qv_bias: float32 [2, 1152], P(None, 'mp'), may hold values from -4 to 4
- proj_weight: bfloat16 [1152, 1152], P('mp'), may hold values from -1.5 to 1.5
- proj_bias: float32 [1152], replicated, may hold values from -4 to 4
- fc1_weight: bfloat16 [1152, 4608], P(None, 'mp'), may hold values from -0.1875 to 0.1875
- fc1_bias: float32 [4608], P('mp'), may hold values from -4 to 4
- fc2_weight: bfloat16 [4608, 1152], P('mp'), may hold values from -0.09375 to 0.09375
- fc2_bias: float32 [1152], replicated, may hold values from -4 to 4
Outputs:
- layer_out: float32 [16384, 1152], P('dp')
- branch_rms: float32 [2, 16384], P(None, 'dp')
- block_input_gradient: float32 [16384, 1152], P('dp')
- time_weight_grad: float32 [256, 1152], P(None, 'mp')
- class_table_grad: float32 [1000, 1152], P(None, 'mp')
- ada_weight_grad: float32 [1152, 6, 1152], P('mp')
- ada_bias_grad: float32 [6, 1152], replicated
- qkv_weight_grad: float32 [3, 1152, 1152], P(None, None, 'mp')
- qv_bias_grad: float32 [2, 1152], P(None, 'mp')
- proj_weight_grad: float32 [1152, 1152], P('mp')
- proj_bias_grad: float32 [1152], replicated
- fc1_weight_grad: float32 [1152, 4608], P(None, 'mp')
- fc1_bias_grad: float32 [4608], P('mp')
- fc2_weight_grad: float32 [4608, 1152], P('mp')
- fc2_bias_grad: float32 [1152], replicated
Inputs may be any that keep to these rules, and one draw needn't show every extreme that they name: Each row holds 1 to 3 crops in its first slots, each of 128 to 512 tokens; unused slots hold 0; a row's lengths and its padding add up to 512.
All inputs are finite; a program needn't handle non-finite values. No bound on the sum of `crop_head_mask` or of `channel_group_mask` or of `token_skip_flag` on one device may be relied on, other than what follows from the above.
Results may differ from a plain program's by a relative error of at most 0.018.
The roundings to bfloat16 on the way count: a program that leaves them out, or rounds other values in their place, can miss the bound.
Values sent between devices are 32-bit elements; how exact they have to be, the bound alone decides.
No kernel may reach another device: no remote copies, remote signals or barrier semaphores. Data moves between devices by JAX's collectives and lax.ppermute only.
A program may use at most 320 MiB of HBM per device.

v0:
```python
import math

import jax
import jax.numpy as jnp
from jax import lax
from jax.sharding import PartitionSpec as P

HEAD_DIM = 72
GROUP_HIDDEN = 288
TFREQ = 256
NCLASS = 1000
CROPS = 3
ROW_LENGTH = 512


highest = lax.Precision.HIGHEST
epsilon = 1e-06


def segments(lengths, padding):
    ends = jnp.cumsum(lengths, axis=1)
    place_tokens = jnp.arange(ROW_LENGTH, dtype=jnp.int32)
    token_count = jnp.sum(
        (place_tokens[None, :, None] >= ends[:, None, :]).astype(jnp.int32), axis=2
    )
    valid_tokens = place_tokens[None, :] < (ROW_LENGTH - padding)[:, None]
    return jnp.where(valid_tokens, token_count, CROPS)


def sinusoid(steps):
    half = TFREQ // 2
    rates = jnp.exp(-math.log(10000.0) * jnp.arange(half, dtype=jnp.float32) / half)
    angles = steps.astype(jnp.float32)[:, None] * rates[None, :]
    return jnp.concatenate([jnp.cos(angles), jnp.sin(angles)], axis=1)


def layer_normalize(value_rows):
    center = value_rows - jnp.mean(value_rows, axis=-1, keepdims=True)
    spread_sq = jnp.mean(center * center, axis=-1, keepdims=True)
    return center * lax.rsqrt(spread_sq + epsilon)


def gelu_tanh(value_rows):
    return (
        0.5
        * value_rows
        * (
            1.0
            + jnp.tanh(
                0.7978845608028654 * (value_rows + 0.044715 * value_rows * value_rows * value_rows)
            )
        )
    )


def silu(value_rows):
    return value_rows / (1.0 + jnp.exp(-value_rows))


def product(left, right):
    return jnp.dot(left, right, preferred_element_type=jnp.float32)


def exact(left, right):
    return jnp.dot(left, right, precision=highest)


def variance(crop_segment, table):
    result = jnp.zeros((crop_segment.shape[0], crop_segment.shape[1], table.shape[2]), jnp.float32)
    for slot in range(CROPS):
        result = jnp.where((crop_segment == slot)[:, :, None], table[:, slot][:, None, :], result)
    return result


def collect(crop_segment, values):
    return jnp.stack(
        [
            jnp.sum(jnp.where((crop_segment == slot)[:, :, None], values, 0.0), axis=1)
            for slot in range(CROPS)
        ],
        axis=1,
    )


def row_scores(query, keys, crop_segment):
    length = query.shape[0]
    query_h = query.reshape(length, -1, HEAD_DIM)
    keys_h = keys.reshape(length, -1, HEAD_DIM)
    scores = jnp.einsum("qhd,khd->hqk", query_h, keys_h, preferred_element_type=jnp.float32) * (
        1.0 / math.sqrt(HEAD_DIM)
    )
    same = crop_segment[:, None] == crop_segment[None, :]
    return (jnp.where(same[None], scores, -1e30), query_h, keys_h)


def attend_forward(pieces):
    query, keys, values, crop_segment = pieces
    length = query.shape[0]
    scores, query_h, keys_h = row_scores(query, keys, crop_segment)
    values_h = values.reshape(length, -1, HEAD_DIM)
    peak = jnp.max(scores, axis=-1, keepdims=True)
    exponent = jnp.exp(scores - peak)
    total = jnp.sum(exponent, axis=-1, keepdims=True)
    probs = (exponent / total).astype(jnp.bfloat16)
    mixed = jnp.einsum("hqk,khd->qhd", probs, values_h, preferred_element_type=jnp.float32)
    return (mixed.reshape(length, -1), (peak + jnp.log(total))[:, :, 0])


def attend_backward(pieces):
    query, keys, values, crop_segment, logsum, upstream = pieces
    length = query.shape[0]
    scores, query_h, keys_h = row_scores(query, keys, crop_segment)
    values_h = values.reshape(length, -1, HEAD_DIM)
    upstream_h = upstream.reshape(length, -1, HEAD_DIM)
    probs = jnp.exp(scores - logsum[:, :, None])
    value_grad = jnp.einsum(
        "hqk,qhd->khd", probs.astype(jnp.bfloat16), upstream_h, preferred_element_type=jnp.float32
    )
    prob_grad = jnp.einsum("qhd,khd->hqk", upstream_h, values_h, preferred_element_type=jnp.float32)
    center = jnp.sum(probs * prob_grad, axis=-1, keepdims=True)
    score_grad = (probs * (prob_grad - center)).astype(jnp.bfloat16)
    scale = 1.0 / math.sqrt(HEAD_DIM)
    query_grad = (
        jnp.einsum("hqk,khd->qhd", score_grad, keys_h, preferred_element_type=jnp.float32) * scale
    )
    key_grad = (
        jnp.einsum("hqk,qhd->khd", score_grad, query_h, preferred_element_type=jnp.float32) * scale
    )
    return (
        query_grad.reshape(length, -1),
        key_grad.reshape(length, -1),
        value_grad.reshape(length, -1),
    )


def shards(
    inputs,
    cotangent,
    lengths,
    padding,
    timesteps,
    classes,
    crop_head_mask,
    channel_group_mask,
    token_skip_flag,
    time_weight,
    class_table,
    ada_weight,
    ada_bias,
    qkv_weight,
    qv_bias,
    proj_weight,
    proj_bias,
    fc1_weight,
    fc1_bias,
    fc2_weight,
    fc2_bias,
):
    row_tokens = lengths.shape[0]
    width = inputs.shape[1]
    local_width = qkv_weight.shape[2]

    def by_rows(value_rows):
        return value_rows.reshape(row_tokens, ROW_LENGTH, -1)

    crop_segment = segments(lengths, padding)
    frequency = sinusoid(timesteps.reshape(-1)).astype(jnp.bfloat16)
    class_hot = (
        classes.reshape(-1)[:, None] == jnp.arange(NCLASS, dtype=jnp.int32)[None, :]
    ).astype(jnp.bfloat16)
    condition = product(frequency, time_weight) + product(class_hot, class_table)
    activated_f, silu_pull = jax.vjp(silu, condition)
    activated = activated_f.astype(jnp.bfloat16)
    partial_mod = product(activated, ada_weight.reshape(local_width, 6 * width))
    modulate = (lax.psum(partial_mod, "mp").reshape(-1, 6, width) + ada_bias).reshape(
        row_tokens, CROPS, 6, width
    )
    first_shift, first_scale, gate_one, second_shift, second_scale, gate_two = [
        variance(crop_segment, modulate[:, :, j]).reshape(-1, width) for j in range(6)
    ]
    head_token_mask = variance(crop_segment, crop_head_mask.astype(jnp.float32)).reshape(
        row_tokens * ROW_LENGTH, -1
    )
    head_cols = jnp.repeat(head_token_mask, HEAD_DIM, axis=1)
    group_cols = jnp.repeat(
        variance(crop_segment, channel_group_mask.astype(jnp.float32)).reshape(
            row_tokens * ROW_LENGTH, -1
        ),
        GROUP_HIDDEN,
        axis=1,
    )
    keep_flags = (1 - token_skip_flag).astype(jnp.float32)[:, None]
    first_normalized, pull_gradient_first = jax.vjp(layer_normalize, inputs)
    first_branch = (first_normalized * (1.0 + first_scale) + first_shift).astype(jnp.bfloat16)
    query = (product(first_branch, qkv_weight[0]) + qv_bias[0]).astype(jnp.bfloat16)
    keys = product(first_branch, qkv_weight[1]).astype(jnp.bfloat16)
    values = (product(first_branch, qkv_weight[2]) + qv_bias[1]).astype(jnp.bfloat16)
    mixed, logsum = lax.map(
        attend_forward, (by_rows(query), by_rows(keys), by_rows(values), crop_segment)
    )
    merged = (mixed.reshape(-1, local_width) * head_cols).astype(jnp.bfloat16)
    branch_attn = lax.psum(product(merged, proj_weight), "mp") + proj_bias
    middle_state = inputs + gate_one * branch_attn
    second_normalized, pull_gradient_second = jax.vjp(layer_normalize, middle_state)
    second_branch = (second_normalized * (1.0 + second_scale) + second_shift).astype(jnp.bfloat16)
    hidden = product(second_branch, fc1_weight) + fc1_bias
    hidden_act, gelu_pull = jax.vjp(gelu_tanh, hidden)
    gated = (hidden_act * group_cols).astype(jnp.bfloat16)
    branch_mlp = lax.psum(product(gated, fc2_weight), "mp") + fc2_bias
    layer_out = middle_state + gate_two * keep_flags * branch_mlp
    branch_rms = jnp.stack(
        [
            jnp.sqrt(jnp.mean(branch_attn * branch_attn, axis=-1) + epsilon),
            jnp.sqrt(jnp.mean(branch_mlp * branch_mlp, axis=-1) + epsilon),
        ]
    )
    mlp_grad = (gate_two * keep_flags * cotangent).astype(jnp.bfloat16)
    fc2_bias_grad = jnp.sum(mlp_grad.astype(jnp.float32), axis=0)
    fc2_weight_grad = product(gated.T, mlp_grad)
    (hidden_pre,) = gelu_pull(product(mlp_grad, fc2_weight.T) * group_cols)
    hidden_grad = hidden_pre.astype(jnp.bfloat16)
    fc1_bias_grad = jnp.sum(hidden_grad.astype(jnp.float32), axis=0)
    fc1_weight_grad = product(second_branch.T, hidden_grad)
    second_branch_gradient = lax.psum(product(hidden_grad, fc1_weight.T), "mp")
    (middle_part,) = pull_gradient_second(second_branch_gradient * (1.0 + second_scale))
    middle_grad = cotangent + middle_part
    attn_grad = (gate_one * middle_grad).astype(jnp.bfloat16)
    proj_bias_grad = jnp.sum(attn_grad.astype(jnp.float32), axis=0)
    proj_weight_grad = product(merged.T, attn_grad)
    mixed_grad = product(attn_grad, proj_weight.T).astype(jnp.bfloat16) * head_cols.astype(
        jnp.bfloat16
    )
    query_pre, key_pre, value_pre = lax.map(
        attend_backward,
        (by_rows(query), by_rows(keys), by_rows(values), crop_segment, logsum, by_rows(mixed_grad)),
    )
    query_grad = query_pre.reshape(-1, local_width).astype(jnp.bfloat16)
    key_grad = key_pre.reshape(-1, local_width).astype(jnp.bfloat16)
    value_grad = value_pre.reshape(-1, local_width).astype(jnp.bfloat16)
    qv_bias_grad = jnp.stack(
        [
            jnp.sum(query_grad.astype(jnp.float32), axis=0),
            jnp.sum(value_grad.astype(jnp.float32), axis=0),
        ]
    )
    qkv_weight_grad = jnp.stack(
        [
            product(first_branch.T, query_grad),
            product(first_branch.T, key_grad),
            product(first_branch.T, value_grad),
        ]
    )
    first_part = (
        product(query_grad, qkv_weight[0].T)
        + product(key_grad, qkv_weight[1].T)
        + product(value_grad, qkv_weight[2].T)
    )
    first_branch_gradient = lax.psum(first_part, "mp")
    (input_part,) = pull_gradient_first(first_branch_gradient * (1.0 + first_scale))
    block_input_gradient = middle_grad + input_part
    token_grads = [
        first_branch_gradient,
        first_branch_gradient * first_normalized,
        middle_grad * branch_attn,
        second_branch_gradient,
        second_branch_gradient * second_normalized,
        cotangent * keep_flags * branch_mlp,
    ]
    modulate_grad = jnp.stack(
        [collect(crop_segment, by_rows(grad_piece)) for grad_piece in token_grads], axis=2
    ).reshape(-1, 6, width)
    ada_bias_grad = jnp.sum(modulate_grad, axis=0)
    flat_grad = modulate_grad.reshape(-1, 6 * width)
    ada_weight_grad = exact(activated.astype(jnp.float32).T, flat_grad).reshape(
        local_width, 6, width
    )
    activated_grad = exact(
        flat_grad, ada_weight.reshape(local_width, 6 * width).astype(jnp.float32).T
    )
    (condition_grad,) = silu_pull(activated_grad)
    time_weight_grad = exact(frequency.astype(jnp.float32).T, condition_grad)
    class_table_grad = exact(class_hot.astype(jnp.float32).T, condition_grad)
    (
        time_weight_grad,
        class_table_grad,
        ada_weight_grad,
        ada_bias_grad,
        qkv_weight_grad,
        qv_bias_grad,
        proj_weight_grad,
        proj_bias_grad,
        fc1_weight_grad,
        fc1_bias_grad,
        fc2_weight_grad,
        fc2_bias_grad,
    ) = lax.psum(
        (
            time_weight_grad,
            class_table_grad,
            ada_weight_grad,
            ada_bias_grad,
            qkv_weight_grad,
            qv_bias_grad,
            proj_weight_grad,
            proj_bias_grad,
            fc1_weight_grad,
            fc1_bias_grad,
            fc2_weight_grad,
            fc2_bias_grad,
        ),
        "dp",
    )
    return (
        layer_out,
        branch_rms,
        block_input_gradient,
        time_weight_grad,
        class_table_grad,
        ada_weight_grad,
        ada_bias_grad,
        qkv_weight_grad,
        qv_bias_grad,
        proj_weight_grad,
        proj_bias_grad,
        fc1_weight_grad,
        fc1_bias_grad,
        fc2_weight_grad,
        fc2_bias_grad,
    )


def solution(mesh):
    in_specs = (
        P("dp", None),
        P("dp", None),
        P("dp", None),
        P("dp"),
        P("dp", None),
        P("dp", None),
        P("dp", None, "mp"),
        P("dp", None, "mp"),
        P("dp"),
        P(None, "mp"),
        P(None, "mp"),
        P("mp", None, None),
        P(),
        P(None, None, "mp"),
        P(None, "mp"),
        P("mp", None),
        P(),
        P(None, "mp"),
        P("mp"),
        P("mp", None),
        P(),
    )
    out_specs = (
        P("dp", None),
        P(None, "dp"),
        P("dp", None),
        P(None, "mp"),
        P(None, "mp"),
        P("mp", None, None),
        P(),
        P(None, None, "mp"),
        P(None, "mp"),
        P("mp", None),
        P(),
        P(None, "mp"),
        P("mp"),
        P("mp", None),
        P(),
    )
    return jax.shard_map(shards, mesh=mesh, in_specs=in_specs, out_specs=out_specs, check_vma=False)
```

profile of v0, /device:TPU:0, one launch (start us, length us, event | category | flops | bytes accessed | tf_op | source)
XLA Modules:
  0.0 2064.7 jit_solution(17609318514695347910)
XLA Ops:
  9.0 2.5 copy.158
  16.7 4.2 reduce_sum.350
  21.0 4.8 multiply_reduce_fusion.6
  26.5 28.7 %all-reduce.9.cloned.1.call-done = f32[4,3,6,1152]{3,2,1,0:T(8,128)} async-done(((f32[4,3,6,1152]{3,2,1,0:T(8,128)}), f32[4,3,6,1152]{3,2,1,0:T(8,128)}) %all-reduce.9.cloned.1.call-update) | async-done | bytes 331792 | tf_op jit(solution)/shard_map/psum | solution.py:175
  57.3 13.6 convert_reduce_fusion
  79.6 76.7 %while.26 = (s32[]{:T(128)}, f32[4,512,288]{1,0,2:T(4,128)}, f32[4,4,512]{2,1,0:T(4,128)}, bf16[4,512,288]{1,2,0:T(8,128)(2,1)}, s32[4,512]{1,0:T(4,128)S(1)}, /...) while((s32[]{:T(128)}, f32[4,512,288]{1,0,2:T(4,128)}, ...), condition=%wide.region_8.9_spmd, body=%wide.region_5.8_spmd.sunk | while | flops 314832896 | bytes 19306616 | solution.py:198
  86.4 12.3 dynamic_update_slice.26
  105.6 12.3 dynamic_update_slice.26
  124.8 12.3 dynamic_update_slice.26
  143.9 12.3 dynamic_update_slice.26
  156.2 2.7 copy.165
  160.2 5.6 fusion.93
  165.9 4.9 broadcast_in_dim.603
  170.8 10.1 copy.103
  183.0 307.6 %all-reduce.11.cloned.1.call-done = f32[2048,1152]{1,0:T(8,128)} async-done(((f32[2048,1152]{1,0:T(8,128)}), f32[2048,1152]{1,0:T(8,128)}) %all-reduce.11.cloned.1.call-update) | async-done | bytes 9437200 | tf_op jit(solution)/shard_map/psum | solution.py:202
  490.6 8.6 fusion.88
  500.4 3.6 copy-done.2
  504.1 21.6 %fusion.20 = bf16[2048,1152]{1,0:T(8,128)(2,1)} fusion(f32[2048,1152]{1,0:T(8,128)S(1)} %get-tuple-element.256, f32[4,1152]{1,0:T(4,128)S(1)} %copy-done.40, f32[4,1152]{1,0:T(4,128)S(1)} %copy-done.41, f32[4,1152]{1,0:T(4,128)S(1)} %copy-done.39, f32[4,1152]{1,0:T(4,128)S(1)} %get-tuple-element.285, f32[4,1152]{1,0:T(4,128)S(1)} %get-tuple-element.286, ...), kind=kLoop, calls=%fused_computation.53 | loop fusion | flops 28311552 | bytes 14288896 | tf_op jit(solution)/shard_map/convert_element_type | solution.py:205
  525.7 12.4 multiply_convert_fusion.1
  538.1 18.6 convert_reduce_fusion.1
  556.7 10.9 fusion.95
  567.8 11.7 fusion.94
  579.5 311.9 %all-reduce.13.cloned.1.call-done = f32[2048,1152]{1,0:T(8,128)} async-done(((f32[2048,1152]{1,0:T(8,128)}), f32[2048,1152]{1,0:T(8,128)}) %all-reduce.13.cloned.1.call-update) | async-done | bytes 9437200 | tf_op jit(solution)/shard_map/psum | solution.py:224
  891.4 10.2 multiply_reduce_fusion.2
  901.7 12.5 fusion.87
  914.3 6.9 convert_reduce_fusion.2
  924.5 50.8 %while.27 = (s32[]{:T(128)}, bf16[4,512,288]{1,2,0:T(8,128)(2,1)}, bf16[4,512,288]{1,2,0:T(8,128)(2,1)}, bf16[4,512,288]{1,2,0:T(8,128)(2,1)}, bf16[4,512,288]{1...) while((s32[]{:T(128)}, bf16[4,512,288]{1,2,0:T(8,128)(2,1)}, ...), condition=%wide.region_20.21_spmd, body=%wide.region_18.20_spmd.sunk | while | flops 771553280 | bytes 39647380 | solution.py:233
  978.5 2.9 fusion.54
  981.4 2.9 convolution_add_fusion.1
  984.3 5.3 convolution_add_fusion
  989.9 12.6 fusion.98
  1002.5 13.0 fusion.99
  1020.6 2.2 pad_maximum_fusion
  1022.9 2.8 fusion.97
  1025.6 593.6 %all-reduce.17.cloned.1.call-done = (f32[2048,1152]{1,0:T(8,128)}, f32[2048,1152]{1,0:T(8,128)}) async-done(((f32[2048,1152]{1,0:T(8,128)}, f32[2048,1152]{1,0:T(8,128)}), (f32[2048,1152]{1,0:T(8,128)}, f32[2048,1152]{1,0:T(8,128)})) %all-reduce.17.cloned.1.call-update) | async-done | bytes 18874384 | tf_op jit(solution)/shard_map/psum | solution.py:209
  1619.3 26.1 %multiply_multiply_fusion.2 = (f32[2048,1152]{1,0:T(8,128)}, f32[2048,1152]{1,0:T(8,128)}, f32[2048]{0:T(1024)S(1)}, f32[2048]{0:T(1024)S(1)}) fusion(f32[2048,1152]{1,0:T(8,128)} %param.26, f32[2048,1152]{1,0:T(8,128)} %get-tuple-element.244, f32[1152]{0:T(1024)S(1)} %copy-done.63, f32[2048]{0:T(1024)S(1)} %copy-done.45, f32[2048,1152]{1,0:T(8,128)} %copy-done.2, ...), kind=kLoop, calls=%fused_computation.92 | loop fusion | flops 44822528 | bytes 66214400 | tf_op jit(solution)/shard_map/mul | solution.py:267
  1645.6 13.2 fusion.86
  1658.8 17.3 add_multiply_fusion
  1676.1 33.8 %select_reduce_fusion.17 = (f32[4,1152]{1,0:T(4,128)S(1)}, f32[4,1152]{1,0:T(4,128)S(1)}, f32[4,1152]{1,0:T(4,128)S(1)}, f32[4,1152]{1,0:T(4,128)S(1)}, f32[4,11...) fusion(pred[4,512]{1,0:T(4,128)(4,1)S(1)} %copy-done.62, ...), kind=kLoop, calls=%fused_computation.107 | loop fusion | flops 84851712 | bytes 56961024 | tf_op jit(solution)/shard_map/reduce_sum | solution.py:78
  1711.0 3.2 fusion.96
  1717.1 5.5 fusion.65
  1725.4 27.3 %all-reduce = (f32[6,1152]{1,0:T(8,128)}, f32[2,288]{1,0:T(2,128)}, f32[1152]{0:T(1024)}, f32[1152]{0:T(1024)}, f32[1152]{0:T(1024)}) all-reduce(f32[6,1152]{1,0:T(8,128)S(1)} %reduce_sum.378, f32[2,288]{1,0:T(2,128)S(1)} %pad_maximum_fusion.11, f32[1152]{0:T(1024)S(1)} %copy-done.55, ...), channel_id=1, replica_groups=mesh['dp'=8,'mp'=4] {'dp'}, use_global_device_ids=true, to_apply=%region_46.47 | all-reduce | flops 10944 | bytes 87552 | tf_op jit(solution)/shard_map/psum | solution.py:296
  1753.3 283.6 %all-reduce.15.cloned.1.call-done = (f32[256,288]{0,1:T(8,128)}, f32[1000,288]{0,1:T(8,128)}, f32[288,6,1152]{2,0,1:T(8,128)}, f32[3,1152,288]{1,2,0:T(8,128)}, ...) async-done(((f32[256,288]{0,1:T(8,128)}, f32[1000,288]{0,1:T(8,128)}, f32[288,6,1152]{2,0,1:T(8,128)}, f32[3,1152,288]{1,2,0:T(8,128)}, ...) | async-done | bytes 25334800 | tf_op jit(solution)/shard_map/psum | solution.py:296
  2038.5 2.6 copy.242
  2041.1 7.2 copy.243
  2048.3 1.9 copy.244
  2051.6 2.7 copy.246
  2055.6 2.4 copy.247
  (437 shorter events, 123.6 us)
Async XLA Ops:
  7.2 518.4 %copy-start = (bf16[1152,1152]{1,0:T(8,128)(2,1)S(1)}, bf16[1152,1152]{1,0:T(8,128)(2,1)}, u32[]{:S(2)}) copy-start(bf16[1152,1152]{1,0:T(8,128)(2,1)} %param.42) | copy-start | bytes 7962628
  7.2 48.0 %all-reduce.9.cloned.1.call-start = ((), (), s32[]{:S(2)}) async-start(), calls=%async_computation | async-start | bytes 884736 | tf_op jit(solution)/shard_map/psum | solution.py:175
  15.0 475.6 %all-reduce.11.cloned.1.call-start = ((), (), s32[]{:S(2)}) async-start(), calls=%async_computation.1 | async-start | bytes 18874368 | tf_op jit(solution)/shard_map/psum | solution.py:202
  16.7 40.5 %copy-start.44 = (f32[2048]{0:T(1024)}, f32[2048]{0:T(1024)S(1)}, u32[]{:S(2)}) copy-start(f32[2048]{0:T(1024)S(1)} %subtract_convert_fusion) | copy-start | bytes 24580
  20.9 34.3 %copy-start.52 = (f32[6,1152]{1,0:T(8,128)S(1)}, f32[6,1152]{1,0:T(8,128)}, u32[]{:S(2)}) copy-start(f32[6,1152]{1,0:T(8,128)} %param.37) | copy-start | bytes 82948
  21.0 36.3 %copy-start.29 = (f32[2048]{0:T(1024)}, f32[2048]{0:T(1024)S(1)}, u32[]{:S(2)}) copy-start(f32[2048]{0:T(1024)S(1)} %broadcast_multiply_fusion.1) | copy-start | bytes 24580
  25.8 29.4 %copy-start.42 = (f32[2048]{0:T(1024)}, f32[2048]{0:T(1024)S(1)}, u32[]{:S(2)}) copy-start(f32[2048]{0:T(1024)S(1)} %multiply_reduce_fusion.6) | copy-start | bytes 24580
  26.5 44.5 %copy-start.46 = (f32[2048]{0:T(1024)}, f32[2048]{0:T(1024)S(1)}, u32[]{:S(2)}) copy-start(f32[2048]{0:T(1024)S(1)} %fusion.76) | copy-start | bytes 24580
  57.1 13.8 copy-start.31
  57.2 13.8 copy-start.33
  57.2 13.8 copy-start.35
  57.2 13.7 copy-start.23
  57.3 13.7 copy-start.25
  57.3 13.7 copy-start.27
  57.3 13.7 copy-start.16
  165.8 725.6 %all-reduce.13.cloned.1.call-start = ((), (), s32[]{:S(2)}) async-start(), calls=%async_computation.2 | async-start | bytes 18874368 | tf_op jit(solution)/shard_map/psum | solution.py:224
  170.8 319.8 %copy-start.53 = (f32[1152]{0:T(1024)S(1)}, f32[1152]{0:T(1024)}, u32[]{:S(2)}) copy-start(f32[1152]{0:T(1024)} %param.41) | copy-start | bytes 13828
  499.3 26.3 %slice-start.6 = ((s8[9437184]{0:T(1024)(128)(4,1)}), s8[4194304]{0:T(1024)(128)(4,1)S(1)}, s32[]{:S(2)}) async-start(s8[9437184]{0:T(1024)(128)(4,1)} %bitcast.548), calls=%async_computation.11 | async-start | bytes 8388608
  499.3 26.3 %slice-start.7 = ((s8[9437184]{0:T(1024)(128)(4,1)}), s8[4194304]{0:T(1024)(128)(4,1)S(1)}, s32[]{:S(2)}) async-start(s8[9437184]{0:T(1024)(128)(4,1)} %bitcast.548), calls=%async_computation.12 | async-start | bytes 8388608
  504.0 21.6 %slice-start.8 = ((s8[9437184]{0:T(1024)(128)(4,1)}), s8[1048576]{0:T(1024)(128)(4,1)S(1)}, s32[]{:S(2)}) async-start(s8[9437184]{0:T(1024)(128)(4,1)} %bitcast.548), calls=%async_computation.13 | async-start | bytes 2097152
  504.0 21.6 %copy-start.72 = (f32[1152]{0:T(1024)S(1)}, f32[1152]{0:T(1024)}, u32[]{:S(2)}) copy-start(f32[1152]{0:T(1024)} %param.43) | copy-start | bytes 13828
  567.6 1051.6 %all-reduce.17.cloned.1.call-start = ((), (), s32[]{:S(2)}) async-start(), calls=%async_computation.4 | async-start | bytes 37748736 | tf_op jit(solution)/shard_map/psum | solution.py:209
  901.6 12.6 slice-start.3
  901.7 12.6 slice-start.4
  901.7 12.6 slice-start.5
  989.6 1047.2 %all-reduce.15.cloned.1.call-start = ((), (), s32[]{:S(2)}) async-start(), calls=%async_computation.3 | async-start | bytes 50724864 | tf_op jit(solution)/shard_map/psum | solution.py:296
  989.8 25.6 %slice-start.15 = ((s8[4718592]{0:T(1024)(128)(4,1)}), s8[4194304]{0:T(1024)(128)(4,1)S(1)}, s32[]{:S(2)}) async-start(s8[4718592]{0:T(1024)(128)(4,1)} %bitcast.567), calls=%async_computation.20 | async-start | bytes 8388608
  1002.5 13.0 slice-start.16
  1022.8 596.4 %copy-start.24 = (f32[4,1152]{1,0:T(4,128)S(1)}, f32[4,1152]{1,0:T(4,128)}, u32[]{:S(2)}) copy-start(f32[4,1152]{1,0:T(4,128)} %copy-done.23) | copy-start | bytes 55300
  1022.8 596.4 %copy-start.26 = (f32[4,1152]{1,0:T(4,128)S(1)}, f32[4,1152]{1,0:T(4,128)}, u32[]{:S(2)}) copy-start(f32[4,1152]{1,0:T(4,128)} %copy-done.25) | copy-start | bytes 55300
  1022.8 596.4 %copy-start.28 = (f32[4,1152]{1,0:T(4,128)S(1)}, f32[4,1152]{1,0:T(4,128)}, u32[]{:S(2)}) copy-start(f32[4,1152]{1,0:T(4,128)} %copy-done.27) | copy-start | bytes 55300
  1022.8 596.4 %copy-start.30 = (f32[2048]{0:T(1024)S(1)}, f32[2048]{0:T(1024)}, u32[]{:S(2)}) copy-start(f32[2048]{0:T(1024)} %copy-done.29) | copy-start | bytes 24580
  1022.8 596.4 %copy-start.32 = (f32[4,1152]{1,0:T(4,128)S(1)}, f32[4,1152]{1,0:T(4,128)}, u32[]{:S(2)}) copy-start(f32[4,1152]{1,0:T(4,128)} %copy-done.31) | copy-start | bytes 55300
  1022.8 596.4 %copy-start.34 = (f32[4,1152]{1,0:T(4,128)S(1)}, f32[4,1152]{1,0:T(4,128)}, u32[]{:S(2)}) copy-start(f32[4,1152]{1,0:T(4,128)} %copy-done.33) | copy-start | bytes 55300
  1022.9 596.4 %copy-start.36 = (f32[4,1152]{1,0:T(4,128)S(1)}, f32[4,1152]{1,0:T(4,128)}, u32[]{:S(2)}) copy-start(f32[4,1152]{1,0:T(4,128)} %copy-done.35) | copy-start | bytes 55300
  1022.9 596.4 %copy-start.45 = (f32[2048]{0:T(1024)S(1)}, f32[2048]{0:T(1024)}, u32[]{:S(2)}) copy-start(f32[2048]{0:T(1024)} %copy-done.44) | copy-start | bytes 24580
  1022.9 596.4 %copy-start.63 = (f32[1152]{0:T(1024)S(1)}, f32[1152]{0:T(1024)}, u32[]{:S(2)}) copy-start(f32[1152]{0:T(1024)} %param.45) | copy-start | bytes 13828
  1619.2 26.3 %slice-start = ((s8[9437184]{0:T(1024)(128)(4,1)}), s8[4194304]{0:T(1024)(128)(4,1)S(1)}, s32[]{:S(2)}) async-start(s8[9437184]{0:T(1024)(128)(4,1)} %bitcast.529), calls=%async_computation.5 | async-start | bytes 8388608
  1619.3 26.2 %copy-start.43 = (f32[2048]{0:T(1024)S(1)}, f32[2048]{0:T(1024)}, u32[]{:S(2)}) copy-start(f32[2048]{0:T(1024)} %copy-done.42) | copy-start | bytes 24580
  1619.3 26.2 %slice-start.1 = ((s8[9437184]{0:T(1024)(128)(4,1)}), s8[4194304]{0:T(1024)(128)(4,1)S(1)}, s32[]{:S(2)}) async-start(s8[9437184]{0:T(1024)(128)(4,1)} %bitcast.529), calls=%async_computation.6 | async-start | bytes 8388608
  1619.3 26.2 %slice-start.2 = ((s8[9437184]{0:T(1024)(128)(4,1)}), s8[1048576]{0:T(1024)(128)(4,1)S(1)}, s32[]{:S(2)}) async-start(s8[9437184]{0:T(1024)(128)(4,1)} %bitcast.529), calls=%async_computation.7 | async-start | bytes 2097152
  1619.3 26.2 %copy-start.47 = (f32[2048]{0:T(1024)S(1)}, f32[2048]{0:T(1024)}, u32[]{:S(2)}) copy-start(f32[2048]{0:T(1024)} %copy-done.46) | copy-start | bytes 24580
  1645.5 13.2 copy-start.54
  1658.7 17.4 copy-start.58
  1658.7 17.4 copy-start.60
  1658.7 17.4 copy-start.62
  1676.1 34.9 %copy-start.5 = (bf16[6,36,8,1152]{3,2,0,1:T(8,128)(2,1)S(1)}, bf16[6,36,8,1152]{3,2,0,1:T(8,128)(2,1)}, u32[]{:S(2)}) copy-start(bf16[6,36,8,1152]{3,2,0,1:T(8,128)(2,1)} %copy-done.4) | copy-start | bytes 11943940
  2038.5 13.1 slice-start.11
  (48 other events, 190.2 us)
Sparse Core Ops, SparseCore 0:
  15.1 40.0 all-reduce.8
  166.0 324.6 all-reduce.10
  567.7 323.6 all-reduce.12
  989.7 629.4 all-reduce.16
  1722.8 313.9 all-reduce.14
where the time goes:
time: 2080 us; the launch traced here: 2060 us
  waiting for transfers between devices  1530 us (74%)
  other arithmetic  194 us (9%)
  matrix products  152 us (7%)
  local copies, waits for them, and re-layouts  149 us (7%)
  blocking collectives  27.3 us (1%)
    psum x1, waiting for transfers between devices, shards(): branch_mlp = lax.psum(product(gated, fc2_weight), 'mp') + fc2_bias  594 us
    psum x1, waiting for transfers between devices, shards(): second_branch_gradient = lax.psum(product(hidden_grad, fc1_weight.T), 'mp')  312 us
    psum x1, waiting for transfers between devices, shards(): branch_attn = lax.psum(product(merged, proj_weight), 'mp') + proj_bias  308 us
    psum x1, waiting for transfers between devices, shards(): lax.psum((time_weight_grad, class_table_grad, ada_weight_grad, ada_bias_g...  284 us
    dot_general x21, matrix products, product(): return jnp.dot(left, right, preferred_element_type=jnp.float32)  112 us
    dynamic_update_slice x16, local copies, waits for them, and re-layouts, shards(): lax.map(attend_forward, (by_rows(query), by_rows(keys), by_rows(values),...  57.8 us
  transfers between devices with their start and end apart: 5, of which 5 were waited for; matrix products, arithmetic and copies ran while one was open for 4% of the time, Pallas kernels for 0%

commit v1 on v0

v1 whole, which is shorter than its diff:
```python
import functools
import math

import jax
import jax.numpy as jnp
from jax import lax
from jax.experimental import pallas as pl
from jax.experimental.pallas import tpu as pltpu
from jax.sharding import PartitionSpec as P

HEAD_DIM = 72
GROUP_HIDDEN = 288
TFREQ = 256
NCLASS = 1000
CROPS = 3
ROW_LENGTH = 512
MIB = 1 << 20

highest = lax.Precision.HIGHEST
epsilon = 1e-06
f32 = jnp.float32
bf16 = jnp.bfloat16
SCALE = 1.0 / math.sqrt(HEAD_DIM)
LOG2E = math.log2(math.e)


def segments(lengths, padding):
    ends = jnp.cumsum(lengths, axis=1)
    place_tokens = jnp.arange(ROW_LENGTH, dtype=jnp.int32)
    token_count = jnp.sum(
        (place_tokens[None, :, None] >= ends[:, None, :]).astype(jnp.int32), axis=2
    )
    valid_tokens = place_tokens[None, :] < (ROW_LENGTH - padding)[:, None]
    return jnp.where(valid_tokens, token_count, CROPS)


def sinusoid(steps):
    half = TFREQ // 2
    rates = jnp.exp(-math.log(10000.0) * jnp.arange(half, dtype=f32) / half)
    angles = steps.astype(f32)[:, None] * rates[None, :]
    return jnp.concatenate([jnp.cos(angles), jnp.sin(angles)], axis=1)


def silu(value_rows):
    return value_rows / (1.0 + jnp.exp(-value_rows))


def product(left, right):
    return jnp.dot(left, right, preferred_element_type=f32)


def exact(left, right):
    return jnp.dot(left, right, precision=highest)


def dot_as(left, right, left_dim, right_dim):
    return lax.dot_general(
        left, right, (((left_dim,), (right_dim,)), ((), ())), preferred_element_type=f32
    )


def tree_sum(values):
    values = list(values)
    while len(values) > 1:
        values = [
            values[i] + values[i + 1] if i + 1 < len(values) else values[i]
            for i in range(0, len(values), 2)
        ]
    return values[0]


def pick(table_ref, j, seg):
    result = jnp.where(seg == 2, table_ref[0, j, 2:3, :], 0.0)
    result = jnp.where(seg == 1, table_ref[0, j, 1:2, :], result)
    return jnp.where(seg == 0, table_ref[0, j, 0:1, :], result)


def normal(rows):
    center = rows - jnp.mean(rows, axis=-1, keepdims=True)
    inverse = lax.rsqrt(jnp.mean(center * center, axis=-1, keepdims=True) + epsilon)
    return center * inverse, inverse


def normal_back(grad, xhat, inverse):
    return (
        grad
        - jnp.mean(grad, axis=-1, keepdims=True)
        - xhat * jnp.mean(grad * xhat, axis=-1, keepdims=True)
    ) * inverse


def crop_sums(values, seg):
    return [
        jnp.sum(jnp.where(seg == slot, values, 0.0), axis=0, keepdims=True) for slot in range(CROPS)
    ]


def first_kernel(x_ref, seg_ref, mod_ref, out_ref):
    xhat, _ = normal(x_ref[...])
    seg = seg_ref[...]
    out_ref[...] = (xhat * (1.0 + pick(mod_ref, 1, seg)) + pick(mod_ref, 0, seg)).astype(bf16)


def attend_kernel(n_pieces, heads, *refs):
    if n_pieces:
        place_ref, refs = refs[0], refs[1:]
    first_ref, segk_ref, segq_ref, mask_ref, bias_ref = refs[:5]
    weight_refs, refs = refs[5 : 5 + max(n_pieces, 1)], refs[5 + max(n_pieces, 1) :]
    if n_pieces:
        qkv_ref, mixed_ref, lse_ref, weight_ref, neg_ref, acc_ref = refs

        @pl.when(pl.program_id(0) == 0)
        def _():
            rows = weight_refs[0].shape[0]
            for m in range(n_pieces):
                at = pl.multiple_of((place_ref[0] ^ m) * rows, 16)
                weight_ref[pl.ds(at, rows), :] = weight_refs[m][...].astype(bf16)
    else:
        qkv_ref, mixed_ref, lse_ref, neg_ref, acc_ref = refs
        weight_ref = weight_refs[0]
    width = heads * HEAD_DIM
    first = first_ref[...]
    for part in range(3):
        rows = pl.ds(part * width, width)
        out = dot_as(weight_ref[rows, :], first, 1, 1) + bias_ref[rows, :]
        for h in range(heads):
            qkv_ref[part * heads + h] = out[h * HEAD_DIM : (h + 1) * HEAD_DIM].astype(bf16)
    neg_ref[...] = jnp.where(segk_ref[...] == segq_ref[0], 0.0, -1e30)
    for h in range(heads):
        query, keys, values = qkv_ref[h], qkv_ref[heads + h], qkv_ref[2 * heads + h]
        scores = dot_as(keys, query, 0, 0) * (SCALE * LOG2E) + neg_ref[...]
        peak = jnp.max(scores, axis=0, keepdims=True)
        exponent = jnp.exp2(scores - peak)
        total = jnp.sum(exponent, axis=0, keepdims=True)
        probs = (exponent * (1.0 / total)).astype(bf16)
        acc_ref[pl.ds(h * HEAD_DIM, HEAD_DIM), :] = (
            dot_as(values, probs, 1, 0) * mask_ref[0, h : h + 1, :]
        )
        lse_ref[0, h : h + 1, :] = peak + jnp.log2(total)
    mixed_ref[...] = acc_ref[...].astype(bf16)


def middle_kernel(parts, hw, *refs):
    mixed_refs, refs = refs[:parts], refs[parts:]
    weight_refs, refs = refs[:parts], refs[parts:]
    (
        bias_ref,
        x_ref,
        cot_ref,
        seg_ref,
        keep_ref,
        mod_ref,
        branch_ref,
        middle_ref,
        second_ref,
        mgrad_ref,
        rms_ref,
        gsum_ref,
    ) = refs
    branch = (
        tree_sum(
            dot_as(mixed_refs[k][...], weight_refs[k][pl.ds(3 * hw, hw), :], 0, 0)
            for k in range(parts)
        )
        + bias_ref[...]
    )
    seg = seg_ref[...]
    branch_ref[...] = branch
    rms_ref[...] = jnp.sqrt(jnp.mean(branch * branch, axis=-1, keepdims=True) + epsilon)
    middle = x_ref[...] + pick(mod_ref, 2, seg) * branch
    middle_ref[...] = middle
    xhat, _ = normal(middle)
    second_ref[...] = (xhat * (1.0 + pick(mod_ref, 4, seg)) + pick(mod_ref, 3, seg)).astype(bf16)
    mgrad = (pick(mod_ref, 5, seg) * keep_ref[...] * cot_ref[...]).astype(bf16)
    mgrad_ref[...] = mgrad

    @pl.when(pl.program_id(0) + pl.program_id(1) == 0)
    def _():
        gsum_ref[...] = jnp.zeros_like(gsum_ref)

    gsum_ref[...] += jnp.sum(mgrad.astype(f32), axis=0, keepdims=True)


def mlp_kernel(n_add, packed, keep_own, *refs):
    second_ref, mgrad_ref, seg_ref, gmask_ref, bias_ref = refs[:5]
    refs = refs[5:]
    if packed:
        pack_ref, refs = refs[0], refs[1:]
    else:
        w1_ref, w2_ref, refs = refs[0], refs[1], refs[2:]
    adds, refs = refs[: 2 * n_add], refs[2 * n_add :]
    bm_ref, sg_ref, refs = refs[0], refs[1], refs[2:]
    if keep_own:
        gated_ref, hgrad_ref, hsum_ref, refs = refs[0], refs[1], refs[2], refs[3:]

        @pl.when(pl.program_id(0) + pl.program_id(1) == 0)
        def _():
            hsum_ref[...] = jnp.zeros_like(hsum_ref)

    if packed:
        w1_ref, w2_ref = refs

        @pl.when(pl.program_id(0) + pl.program_id(1) == 0)
        def _():
            rows = w1_ref.shape[0] // packed
            for d in range(packed):
                w1_ref[pl.ds(d * rows, rows), :] = pack_ref[pl.ds(2 * d * rows, rows), :].astype(bf16)
                w2_ref[pl.ds(d * rows, rows), :] = pack_ref[
                    pl.ds((2 * d + 1) * rows, rows), :
                ].astype(bf16)

    second, mgrad, seg = second_ref[...], mgrad_ref[...], seg_ref[...]
    units = w1_ref.shape[0]
    bm = sg = None
    for at in range(0, units, 512):
        cols = slice(at, min(at + 512, units))
        u = dot_as(second, w1_ref[cols, :], 1, 1) + bias_ref[:, cols]
        up = dot_as(mgrad, w2_ref[cols, :], 1, 1)
        mask = jnp.where(seg == 2, gmask_ref[0, 2:3, cols], 0.0)
        mask = jnp.where(seg == 1, gmask_ref[0, 1:2, cols], mask)
        mask = jnp.where(seg == 0, gmask_ref[0, 0:1, cols], mask)
        square = u * u
        t = jnp.tanh(0.7978845608028654 * u * (1.0 + 0.044715 * square))
        half = 0.5 * (1.0 + t)
        slope = half + (0.5 * u) * (1.0 - t * t) * (
            0.7978845608028654 + (3.0 * 0.044715 * 0.7978845608028654) * square
        )
        gated = (u * half * mask).astype(bf16)
        hgrad = (up * mask * slope).astype(bf16)
        if keep_own:
            gated_ref[:, cols] = gated
            hgrad_ref[:, cols] = hgrad
            hsum_ref[:, cols] += jnp.sum(hgrad.astype(f32), axis=0, keepdims=True)
        bm_part = dot_as(gated, w2_ref[cols, :], 1, 0)
        sg_part = dot_as(hgrad, w1_ref[cols, :], 1, 0)
        bm = bm_part if bm is None else bm + bm_part
        sg = sg_part if sg is None else sg + sg_part
    for i in range(n_add):
        bm = bm + adds[2 * i][...]
        sg = sg + adds[2 * i + 1][...]
    bm_ref[...] = bm
    sg_ref[...] = sg


def turn_kernel(
    middle_ref,
    branch_ref,
    bm_ref,
    sg_ref,
    cot_ref,
    seg_ref,
    keep_ref,
    mod_ref,
    bias_ref,
    out_ref,
    mg_ref,
    ag_ref,
    rms_ref,
    sums_ref,
    asum_ref,
):
    seg, keep, cot = seg_ref[...], keep_ref[...], cot_ref[...]
    bm = bm_ref[...] + bias_ref[...]
    rms_ref[...] = jnp.sqrt(jnp.mean(bm * bm, axis=-1, keepdims=True) + epsilon)
    middle = middle_ref[...]
    kept = keep * bm
    out_ref[...] = middle + pick(mod_ref, 5, seg) * kept
    xhat, inverse = normal(middle)
    sg = sg_ref[...]
    mg = cot + normal_back(sg * (1.0 + pick(mod_ref, 4, seg)), xhat, inverse)
    mg_ref[...] = mg
    ag = (pick(mod_ref, 2, seg) * mg).astype(bf16)
    ag_ref[...] = ag

    @pl.when(pl.program_id(1) == 0)
    def _():
        sums_ref[...] = jnp.zeros_like(sums_ref)

    @pl.when(pl.program_id(0) + pl.program_id(1) == 0)
    def _():
        asum_ref[...] = jnp.zeros_like(asum_ref)

    asum_ref[...] += jnp.sum(ag.astype(f32), axis=0, keepdims=True)
    for j, values in enumerate((mg * branch_ref[...], sg, sg * xhat, cot * kept)):
        for slot, row in enumerate(crop_sums(values, seg)):
            sums_ref[0, j, slot : slot + 1, :] += row


def attend_back_kernel(parts, heads, *refs):
    ag_ref, first_ref, mixed_ref, segk_ref, segq_ref = refs[:5]
    refs = refs[5:]
    mask_refs, refs = refs[:parts], refs[parts:]
    lse_refs, refs = refs[:parts], refs[parts:]
    qkv_refs, refs = refs[:parts], refs[parts:]
    weight_refs, refs = refs[:parts], refs[parts:]
    fg_ref, wgrad_ref, bsum_ref, neg_ref, up_ref, acc_ref = refs
    width = heads * HEAD_DIM
    neg_ref[...] = jnp.where(segk_ref[...] == segq_ref[0], 0.0, -1e30)
    ag = ag_ref[...]

    @pl.when(pl.program_id(0) == 0)
    def _():
        wgrad_ref[...] = jnp.zeros_like(wgrad_ref)
        bsum_ref[...] = jnp.zeros_like(bsum_ref)

    grads = []
    for k in range(parts):
        up = dot_as(weight_refs[k][pl.ds(3 * width, width), :], ag, 1, 1)
        for h in range(heads):
            mask = mask_refs[k][0, h : h + 1, :]
            up_ref[h] = (up[h * HEAD_DIM : (h + 1) * HEAD_DIM].astype(bf16).astype(f32) * mask).astype(bf16)
        for h in range(heads):
            query, keys, values = (qkv_refs[k][i * heads + h] for i in range(3))
            upstream = up_ref[h]
            scores = dot_as(keys, query, 0, 0) * (SCALE * LOG2E) + neg_ref[...]
            probs = jnp.exp2(scores - lse_refs[k][0, h : h + 1, :])
            prob_grad = dot_as(values, upstream, 0, 0)
            center = jnp.sum(probs * prob_grad, axis=0, keepdims=True)
            score_grad = (probs * (prob_grad - center)).astype(bf16)
            at = h * HEAD_DIM
            acc_ref[pl.ds(at, HEAD_DIM), :] = dot_as(keys, score_grad, 1, 0) * SCALE
            acc_ref[pl.ds(width + at, HEAD_DIM), :] = dot_as(query, score_grad, 1, 1) * SCALE
            acc_ref[pl.ds(2 * width + at, HEAD_DIM), :] = dot_as(upstream, probs.astype(bf16), 1, 1)
        back = acc_ref[...].astype(bf16)
        grads.append(dot_as(back, weight_refs[k][pl.ds(0, 3 * width), :], 0, 0))
        if k == 0:
            wgrad_ref[pl.ds(0, 3 * width), :] += dot_as(back, first_ref[...], 1, 0)
            wgrad_ref[pl.ds(3 * width, width), :] += dot_as(mixed_ref[...], ag, 1, 0)
            bsum_ref[...] += jnp.sum(back.astype(f32), axis=1, keepdims=True)
    fg_ref[...] = tree_sum(grads)


def last_kernel(x_ref, fg_ref, mg_ref, seg_ref, mod_ref, out_ref, sums_ref):
    seg = seg_ref[...]
    xhat, inverse = normal(x_ref[...])
    fg = fg_ref[...]
    out_ref[...] = mg_ref[...] + normal_back(fg * (1.0 + pick(mod_ref, 1, seg)), xhat, inverse)

    @pl.when(pl.program_id(1) == 0)
    def _():
        sums_ref[...] = jnp.zeros_like(sums_ref)

    for j, values in enumerate((fg, fg * xhat)):
        for slot, row in enumerate(crop_sums(values, seg)):
            sums_ref[0, j, slot : slot + 1, :] += row


def call(kernel, name, grid, ins, outs, scratch=(), prefetch=(), cost=None, aliases=None, vmem=58):
    arrays = [a for a, _ in ins]
    return pl.pallas_call(
        kernel,
        name=name,
        grid_spec=pltpu.PrefetchScalarGridSpec(
            num_scalar_prefetch=len(prefetch),
            grid=grid,
            in_specs=[s for _, s in ins],
            out_specs=[s for _, s in outs],
            scratch_shapes=list(scratch),
        ),
        out_shape=[a for a, _ in outs],
        input_output_aliases=aliases or {},
        cost_estimate=cost,
        compiler_params=pltpu.CompilerParams(
            dimension_semantics=("arbitrary",) * len(grid), vmem_limit_bytes=vmem * MIB
        ),
    )(*prefetch, *arrays)


def cost_of(flops, moved, transcendentals=0):
    return pl.CostEstimate(
        flops=int(flops), bytes_accessed=int(moved), transcendentals=int(transcendentals)
    )


def whole(array):
    nd = array.ndim
    return (array, pl.BlockSpec(array.shape, lambda *_: (0,) * nd, pipeline_mode=pl.Buffered(1)))


def shape(dims, kind=f32):
    return jax.ShapeDtypeStruct(tuple(dims), kind)


def shards(
    dp_size,
    mp_size,
    inputs,
    cotangent,
    lengths,
    padding,
    timesteps,
    classes,
    crop_head_mask,
    channel_group_mask,
    token_skip_flag,
    time_weight,
    class_table,
    ada_weight,
    ada_bias,
    qkv_weight,
    qv_bias,
    proj_weight,
    proj_bias,
    fc1_weight,
    fc1_bias,
    fc2_weight,
    fc2_bias,
):
    rows = lengths.shape[0]
    tokens, width = inputs.shape
    hw = qkv_weight.shape[2]
    heads = hw // HEAD_DIM
    units = fc2_weight.shape[0]
    groups = channel_group_mask.shape[2]
    place = lax.axis_index("dp")
    mine = lax.axis_index("mp")

    def across_mp(x, k):
        return lax.ppermute(x, "mp", [(i, i ^ k) for i in range(mp_size)])

    def across_dp(x, m):
        return lax.ppermute(x, "dp", [(i, i ^ m) for i in range(dp_size)])

    attn_own = jnp.concatenate(
        [jnp.swapaxes(qkv_weight, 1, 2).reshape(3 * hw, width), proj_weight], axis=0
    )
    fc1_own = fc1_weight.T
    ring = dp_size == 8 and (4 * hw) % (16 * dp_size) == 0 and units % (16 * dp_size) == 0
    attn_parts, mlp_parts = [attn_own], [(fc1_own, fc2_weight)]
    if ring:
        a_rows, m_rows = 4 * hw // dp_size, units // dp_size
        a_slice = lax.dynamic_slice_in_dim(attn_own, place * a_rows, a_rows).astype(f32)
        m_slice = jnp.concatenate(
            [
                lax.dynamic_slice_in_dim(fc1_own, place * m_rows, m_rows),
                lax.dynamic_slice_in_dim(fc2_weight, place * m_rows, m_rows),
            ]
        ).astype(f32)
        for k in range(1, mp_size):
            piece = across_mp(a_slice, k)
            near, far = (2, 4) if k % 2 else (4, 2)
            side = across_dp(piece, near)
            plane = {0: piece, near: side, far: across_dp(piece, far), 6: across_dp(side, far)}
            for m in (0, 2, 4, 6):
                plane[m + 1] = across_dp(plane[m], 1)
            attn_parts.append([plane[m] for m in range(8)])
        for k in range(1, mp_size):
            mlp_parts.append(lax.all_gather(across_mp(m_slice, k), "dp", tiled=True))
    else:
        attn_all = lax.all_gather(attn_own.astype(f32), "mp")
        fc1_all = lax.all_gather(fc1_own.astype(f32), "mp")
        fc2_all = lax.all_gather(fc2_weight.astype(f32), "mp")

        def take(stack, k):
            block = (1,) + stack.shape[1:]
            return call(
                lambda _, x_ref, out_ref: out_ref.__setitem__(..., x_ref[0].astype(bf16)),
                "narrow",
                (1,),
                [(stack, pl.BlockSpec(block, lambda i, at: (at[0], 0, 0)))],
                [(shape(stack.shape[1:], bf16), pl.BlockSpec(stack.shape[1:], lambda i, at: (0, 0)))],
                prefetch=[(mine ^ k).reshape(1)],
            )[0]

        for k in range(1, mp_size):
            attn_parts.append(take(attn_all, k))
            mlp_parts.append((take(fc1_all, k), take(fc2_all, k)))

    seg = segments(lengths, padding)
    many = rows * CROPS
    keys_all = lax.all_gather(
        jnp.stack([timesteps.reshape(-1), classes.reshape(-1)]), "dp", axis=1, tiled=True
    )

    def conditioned(steps, labels):
        frequency = sinusoid(steps).astype(bf16)
        class_hot = (labels[:, None] == jnp.arange(NCLASS, dtype=jnp.int32)[None, :]).astype(bf16)
        condition = product(frequency, time_weight) + product(class_hot, class_table)
        return frequency, class_hot, condition

    _, _, condition = conditioned(timesteps.reshape(-1), classes.reshape(-1))
    activated = silu(condition).astype(bf16)
    flat_ada = ada_weight.reshape(hw, 6 * width)
    modulate = lax.psum(product(activated, flat_ada), "mp").reshape(many, 6, width) + ada_bias
    table = jnp.pad(
        modulate.reshape(rows, CROPS, 6, width).transpose(0, 2, 1, 3),
        ((0, 0), (0, 0), (0, 8 - CROPS), (0, 0)),
    )

    n_head, n_group = rows * CROPS * heads, rows * CROPS * groups
    aux_own = jnp.concatenate(
        [
            crop_head_mask.astype(f32).reshape(-1),
            channel_group_mask.astype(f32).reshape(-1),
            qv_bias[0],
            jnp.zeros((hw,), f32),
            qv_bias[1],
            fc1_bias,
        ]
    )
    aux = [aux_own] + [across_mp(aux_own, k) for k in range(1, mp_size)]
    seg_col = seg.reshape(tokens, 1)
    seg_row = seg.reshape(rows, 1, ROW_LENGTH)
    keep_col = (1 - token_skip_flag).astype(f32).reshape(tokens, 1)
    head_masks, group_masks, qkv_biases, fc1_biases = [], [], [], []
    for part in aux:
        head = part[:n_head].reshape(rows, CROPS, heads)
        group = part[n_head : n_head + n_group].reshape(rows, CROPS, groups)
        rest = part[n_head + n_group :]
        by_slot = [
            jnp.where(seg_row == slot, head[:, slot, :, None], 0.0) for slot in range(CROPS)
        ]
        head_masks.append(sum(by_slot))
        group_masks.append(
            jnp.pad(jnp.repeat(group, GROUP_HIDDEN, axis=2), ((0, 0), (0, 8 - CROPS), (0, 0)))
        )
        qkv_biases.append(rest[: 3 * hw].reshape(3 * hw, 1))
        fc1_biases.append(rest[3 * hw :].reshape(1, units))

    tile = 256
    per_row = ROW_LENGTH // tile

    def tok(kind, cols=width):
        return (
            shape((tokens, cols), kind),
            pl.BlockSpec((tile, cols), lambda r, i: (r * per_row + i, 0)),
        )

    def tok_in(array):
        return (
            array,
            pl.BlockSpec((tile, array.shape[1]), lambda r, i: (r * per_row + i, 0)),
        )

    def once(dims, kind=f32):
        nd = len(dims)
        return (shape(dims, kind), pl.BlockSpec(dims, lambda *_: (0,) * nd))

    table_in = (table, pl.BlockSpec((1, 6, 8, width), lambda r, i: (r, 0, 0, 0)))
    grid2 = (rows, per_row)
    grid1 = (rows,)

    def row_in(array, dims):
        nd = len(dims)
        return (array, pl.BlockSpec(dims, lambda r, *_: (r,) + (0,) * (nd - 1)))

    def lane_in(array, dims):
        nd = len(dims)
        return (array, pl.BlockSpec(dims, lambda r, *_: (0,) * (nd - 1) + (r,)))

    (first,) = call(
        first_kernel,
        "first",
        grid2,
        [tok_in(inputs), tok_in(seg_col), table_in],
        [tok(bf16)],
        cost=cost_of(20 * tokens * width, 6 * tokens * width),
    )

    pair = tokens * ROW_LENGTH * heads
    qkv_t, mixed_t, lse, attn_w = [], [], [], []
    for k in range(mp_size):
        part = attn_parts[k]
        pieces = part if isinstance(part, list) else [part]
        n_pieces = len(part) if isinstance(part, list) else 0
        outs = [
            lane_in(shape((3 * heads, HEAD_DIM, tokens), bf16), (3 * heads, HEAD_DIM, ROW_LENGTH)),
            lane_in(shape((hw, tokens), bf16), (hw, ROW_LENGTH)),
            row_in(shape((rows, heads, ROW_LENGTH)), (1, heads, ROW_LENGTH)),
        ]
        if n_pieces:
            outs.append(once((4 * hw, width), bf16))
        result = call(
            functools.partial(attend_kernel, n_pieces, heads),
            "attend",
            grid1,
            [
                row_in(first, (ROW_LENGTH, width)),
                row_in(seg_col, (ROW_LENGTH, 1)),
                row_in(seg_row, (1, 1, ROW_LENGTH)),
                row_in(head_masks[k], (1, heads, ROW_LENGTH)),
                whole(qkv_biases[k]),
            ]
            + [whole(p) for p in pieces],
            outs,
            scratch=[
                pltpu.VMEM((ROW_LENGTH, ROW_LENGTH), f32),
                pltpu.VMEM((hw, ROW_LENGTH), f32),
            ],
            prefetch=[place.reshape(1)] if n_pieces else [],
            cost=cost_of(
                2 * tokens * width * 3 * hw + 4 * pair * HEAD_DIM,
                2 * tokens * width + 8 * tokens * hw + 4 * 4 * hw * width,
                pair,
            ),
        )
        qkv_t.append(result[0])
        mixed_t.append(result[1])
        lse.append(result[2])
        attn_w.append(result[3] if n_pieces else part)

    branch, middle, second, mlp_grad, rms_one, fc2_bias_sum = call(
        functools.partial(middle_kernel, mp_size, hw),
        "middle",
        grid2,
        [
            (m, pl.BlockSpec((hw, tile), lambda r, i: (0, r * per_row + i))) for m in mixed_t
        ]
        + [whole(w) for w in attn_w]
        + [
            whole(proj_bias.reshape(1, width)),
            tok_in(inputs),
            tok_in(cotangent),
            tok_in(seg_col),
            tok_in(keep_col),
            table_in,
        ],
        [tok(f32), tok(f32), tok(bf16), tok(bf16), tok(f32, 1), once((1, width))],
        cost=cost_of(2 * tokens * width * hw * mp_size, 22 * tokens * width),
    )

    stack = []
    gated = hidden_grad = fc1_bias_sum = None
    for k in range(mp_size):
        part = mlp_parts[k]
        packed = 0 if isinstance(part, tuple) else dp_size
        merged = []
        level = 0
        while stack and stack[-1][0] == level:
            merged.append(stack.pop()[1])
            level += 1
        outs = [tok(f32), tok(f32)]
        if k == 0:
            outs += [tok(bf16, units), tok(bf16, units), once((1, units))]
        n_in = 5 + (1 if packed else 2)
        result = call(
            functools.partial(mlp_kernel, len(merged), packed, k == 0),
            "mlp",
            grid2,
            [
                tok_in(second),
                tok_in(mlp_grad),
                tok_in(seg_col),
                (group_masks[k], pl.BlockSpec((1, 8, units), lambda r, i: (r, 0, 0))),
                whole(fc1_biases[k]),
            ]
            + ([whole(part)] if packed else [whole(w) for w in part])
            + [tok_in(a) for pair_of in merged for a in pair_of],
            outs,
            scratch=[pltpu.VMEM((units, width), bf16)] * 2 if packed else [],
            aliases={n_in: 0, n_in + 1: 1} if merged else {},
            cost=cost_of(8 * tokens * width * units, 20 * tokens * width, tokens * units),
        )
        stack.append((level, (result[0], result[1])))
        if k == 0:
            gated, hidden_grad, fc1_bias_sum = result[2:]
    ((_, (branch_mlp, second_grad)),) = stack

    layer_out, middle_grad, attn_grad, rms_two, sums_mid, proj_bias_sum = call(
        turn_kernel,
        "turn",
        grid2,
        [
            tok_in(middle),
            tok_in(branch),
            tok_in(branch_mlp),
            tok_in(second_grad),
            tok_in(cotangent),
            tok_in(seg_col),
            tok_in(keep_col),
            table_in,
            whole(fc2_bias.reshape(1, width)),
        ],
        [
            tok(f32),
            tok(f32),
            tok(bf16),
            tok(f32, 1),
            (shape((rows, 4, 8, width)), pl.BlockSpec((1, 4, 8, width), lambda r, i: (r, 0, 0, 0))),
            once((1, width)),
        ],
        cost=cost_of(60 * tokens * width, 30 * tokens * width),
    )

    fc2_weight_grad = dot_as(gated, mlp_grad, 0, 0)
    fc1_weight_grad = dot_as(second, hidden_grad, 0, 0)

    first_grad, attn_w_grad, qkv_bias_sum = call(
        functools.partial(attend_back_kernel, mp_size, heads),
        "attend_back",
        grid1,
        [
            row_in(attn_grad, (ROW_LENGTH, width)),
            row_in(first, (ROW_LENGTH, width)),
            lane_in(mixed_t[0], (hw, ROW_LENGTH)),
            row_in(seg_col, (ROW_LENGTH, 1)),
            row_in(seg_row, (1, 1, ROW_LENGTH)),
        ]
        + [row_in(m, (1, heads, ROW_LENGTH)) for m in head_masks]
        + [row_in(v, (1, heads, ROW_LENGTH)) for v in lse]
        + [lane_in(q, (3 * heads, HEAD_DIM, ROW_LENGTH)) for q in qkv_t]
        + [whole(w) for w in attn_w],
        [
            row_in(shape((tokens, width)), (ROW_LENGTH, width)),
            once((4 * hw, width)),
            once((3 * hw, 1)),
        ],
        scratch=[
            pltpu.VMEM((ROW_LENGTH, ROW_LENGTH), f32),
            pltpu.VMEM((heads, HEAD_DIM, ROW_LENGTH), bf16),
            pltpu.VMEM((3 * hw, ROW_LENGTH), f32),
        ],
        cost=cost_of(
            mp_size * (8 * tokens * width * hw + 10 * pair * HEAD_DIM),
            20 * tokens * width,
            mp_size * pair,
        ),
    )

    block_input_gradient, sums_first = call(
        last_kernel,
        "last",
        grid2,
        [tok_in(inputs), tok_in(first_grad), tok_in(middle_grad), tok_in(seg_col), table_in],
        [
            tok(f32),
            (shape((rows, 2, 8, width)), pl.BlockSpec((1, 2, 8, width), lambda r, i: (r, 0, 0, 0))),
        ],
        cost=cost_of(40 * tokens * width, 16 * tokens * width),
    )

    local_grad = (
        jnp.concatenate([sums_first, sums_mid], axis=1)[:, :, :CROPS]
        .transpose(0, 2, 1, 3)
        .reshape(many, 6 * width)
    )
    flat_grad = lax.all_gather(local_grad, "dp", tiled=True)
    frequency, class_hot, condition_all = conditioned(keys_all[0], keys_all[1])
    activated_f, silu_pull = jax.vjp(silu, condition_all)
    activated_all = activated_f.astype(bf16)
    ada_bias_grad = jnp.sum(flat_grad, axis=0).reshape(6, width)
    ada_weight_grad = exact(activated_all.astype(f32).T, flat_grad).reshape(hw, 6, width)
    activated_grad = exact(flat_grad, flat_ada.astype(f32).T)
    (condition_grad,) = silu_pull(activated_grad)
    time_weight_grad = exact(frequency.astype(f32).T, condition_grad)
    class_table_grad = exact(class_hot.astype(f32).T, condition_grad)

    fc2_weight_grad, fc1_weight_grad = lax.psum((fc2_weight_grad, fc1_weight_grad), "dp")
    attn_w_grad, qkv_bias_sum, proj_bias_sum, fc1_bias_sum, fc2_bias_sum = lax.psum(
        (
            attn_w_grad,
            qkv_bias_sum.reshape(3, hw),
            proj_bias_sum.reshape(width),
            fc1_bias_sum.reshape(units),
            fc2_bias_sum.reshape(width),
        ),
        "dp",
    )
    qkv_weight_grad = jnp.swapaxes(attn_w_grad[: 3 * hw].reshape(3, hw, width), 1, 2)
    return (
        layer_out,
        jnp.concatenate([rms_one, rms_two], axis=1).T,
        block_input_gradient,
        time_weight_grad,
        class_table_grad,
        ada_weight_grad,
        ada_bias_grad,
        qkv_weight_grad,
        jnp.stack([qkv_bias_sum[0], qkv_bias_sum[2]]),
        attn_w_grad[3 * hw :],
        proj_bias_sum,
        fc1_weight_grad,
        fc1_bias_sum,
        fc2_weight_grad,
        fc2_bias_sum,
    )


def solution(mesh):
    in_specs = (
        P("dp", None),
        P("dp", None),
        P("dp", None),
        P("dp"),
        P("dp", None),
        P("dp", None),
        P("dp", None, "mp"),
        P("dp", None, "mp"),
        P("dp"),
        P(None, "mp"),
        P(None, "mp"),
        P("mp", None, None),
        P(),
        P(None, None, "mp"),
        P(None, "mp"),
        P("mp", None),
        P(),
        P(None, "mp"),
        P("mp"),
        P("mp", None),
        P(),
    )
    out_specs = (
        P("dp", None),
        P(None, "dp"),
        P("dp", None),
        P(None, "mp"),
        P(None, "mp"),
        P("mp", None, None),
        P(),
        P(None, None, "mp"),
        P(None, "mp"),
        P("mp", None),
        P(),
        P(None, "mp"),
        P("mp"),
        P("mp", None),
        P(),
    )
    body = functools.partial(shards, mesh.shape["dp"], mesh.shape["mp"])
    return jax.shard_map(body, mesh=mesh, in_specs=in_specs, out_specs=out_specs, check_vma=False)
```

time: 2080 us -> 1050 us (0.50)
  waiting for transfers between devices: 1530 us -> 387 us
  Pallas kernels: 0 us -> 435 us
  other arithmetic: 194 us -> 13.1 us
  matrix products: 152 us -> 42.4 us
  local copies, waits for them, and re-layouts: 149 us -> 55.1 us
  starting transfers between devices: 0.38 us -> 55.7 us
    psum x5 -> x2, waiting for transfers between devices: 1530 us -> 161 us  [the longest x1 161 us: shards(): lax.psum((attn_w_grad, qkv_bias_sum.reshape(3, hw), proj_bias_sum.reshape...]
    pallas_call x0 -> x13, Pallas kernels: none -> 435 us  [call(): pl.pallas_call(kernel, name=name, grid_spec=pltpu.PrefetchScalarGridSpec(...]
    ppermute x0 -> x30, waiting for transfers between devices: none -> 226 us  [the longest x9 158 us: across_mp(): return lax.ppermute(x, 'mp', [(i, i ^ k) for i in range(mp_size)])]
    reduce_sum x17 -> x1, other arithmetic: 113 us -> 2.33 us  [shards(): ada_bias_grad = jnp.sum(flat_grad, axis=0).reshape(6, width)]
    dot_general x49 -> x6, matrix products: 141 us -> 29.9 us  [the longest x2 25.2 us: dot_as(): lax.dot_general(left, right, (((left_dim,), (right_dim,)), ((), ())), pre...]
    dynamic_update_slice x16 -> x0, local copies, waits for them, and re-layouts: 57.8 us -> none  [shards(): lax.map(attend_forward, (by_rows(query), by_rows(keys), by_rows(values),...]
    ppermute x0 -> x30, starting transfers between devices: none -> 55.4 us  [the longest x9 42.9 us: across_mp(): return lax.ppermute(x, 'mp', [(i, i ^ k) for i in range(mp_size)])]
    mul x2 -> x0, other arithmetic: 43.5 us -> none  [the longest x1 26.1 us: shards(): cotangent * keep_flags * branch_mlp]
  transfers between devices with their start and end apart: 5 -> 36, of which waited for: 5 -> 10; matrix products, arithmetic and copies ran while one was open for 4% -> 8% of each run, Pallas kernels for 0% -> 22%
where the time goes in v1:
time: 1050 us; the launch traced here: 1040 us
  Pallas kernels  435 us (41%)
  waiting for transfers between devices  387 us (37%)
  starting transfers between devices  55.7 us (5%)
  local copies, waits for them, and re-layouts  55.1 us (5%)
  matrix products  42.4 us (4%)
  blocking collectives  34.3 us (3%)
  between operations  16.6 us (2%)
  other arithmetic  13.1 us (1%)
    pallas_call x13, Pallas kernels, call(): pl.pallas_call(kernel, name=name, grid_spec=pltpu.PrefetchScalarGridSpec(...  435 us
    psum x1, waiting for transfers between devices, shards(): lax.psum((attn_w_grad, qkv_bias_sum.reshape(3, hw), proj_bias_sum.reshape...  161 us
    ppermute x9, waiting for transfers between devices, across_mp(): return lax.ppermute(x, 'mp', [(i, i ^ k) for i in range(mp_size)])  158 us
    ppermute x21, waiting for transfers between devices, across_dp(): return lax.ppermute(x, 'dp', [(i, i ^ m) for i in range(dp_size)])  68 us
    ppermute x9, starting transfers between devices, across_mp(): return lax.ppermute(x, 'mp', [(i, i ^ k) for i in range(mp_size)])  42.9 us
    psum x1, blocking collectives, shards(): lax.psum((attn_w_grad, qkv_bias_sum.reshape(3, hw), proj_bias_sum.reshape...  25.4 us
    dot_general x2, matrix products, dot_as(): lax.dot_general(left, right, (((left_dim,), (right_dim,)), ((), ())), pre...  25.2 us
  transfers between devices with their start and end apart: 36, of which 10 were waited for; matrix products, arithmetic and copies ran while one was open for 8% of the time, Pallas kernels for 22%

profile of v1, /device:TPU:0, one launch (start us, length us, event | category | flops | bytes accessed | tf_op | source)
XLA Modules:
  0.0 1039.4 jit_solution(477921478599303798)
XLA Ops:
  8.1 4.2 copy.138
  14.7 4.0 collective-permute-start.28
  18.9 4.4 copy.159
  24.3 3.9 fusion.14
  28.3 1.9 reshape.344
  30.2 1.9 copy.122
  32.1 51.9 %collective-permute-done.28 = f32[288,1152]{1,0:T(8,128)} collective-permute-done((f32[288,1152]{1,0:T(8,128)}, f32[288,1152]{1,0:T(8,128)}, u32[]{:S(2)}, u32[]{:S(2)}) %collective-permute-start.28) | collective-permute-done | bytes 1327136 | tf_op jit(solution)/shard_map/ppermute | solution.py:419
  84.7 37.1 %collective-permute-done.29 = f32[288,1152]{1,0:T(8,128)} collective-permute-done((f32[288,1152]{1,0:T(8,128)}, f32[288,1152]{1,0:T(8,128)}, u32[]{:S(2)}, u32[]{:S(2)}) %collective-permute-start.29) | collective-permute-done | bytes 1327136 | tf_op jit(solution)/shard_map/ppermute | solution.py:419
  121.9 4.2 collective-permute-start.27
  126.1 28.8 %collective-permute-done.27 = f32[288,1152]{1,0:T(8,128)} collective-permute-done((f32[288,1152]{1,0:T(8,128)}, f32[288,1152]{1,0:T(8,128)}, u32[]{:S(2)}, u32[]{:S(2)}) %collective-permute-start.27) | collective-permute-done | bytes 1327136 | tf_op jit(solution)/shard_map/ppermute | solution.py:419
  155.3 29.4 %collective-permute-start.9 = (f32[2112]{0:T(1024)S(1)}, f32[2112]{0:T(1024)S(1)}, u32[]{:S(2)}, u32[]{:S(2)}) collective-permute-start(f32[2112]{0:T(1024)S(1)} %concatenate.30), channel_id=1, source_target_pairs={{0,2},{1,3},{2,0},{3,1},{4,6},{5,7},{6,4},{7,5},{8,10},{9,11},{10,... | collective-permute-start | bytes 25352 | tf_op jit(solution)/shard_map/ppermute | solution.py:419
  187.0 2.6 collective-permute-start.19
  191.6 1.7 pad_maximum_fusion.refs_5_.refs_4_.refs_17_
  193.3 38.4 %collective-permute-done.10.refs_6_ = f32[144,1152]{1,0:T(8,128)} collective-permute-done((f32[144,1152]{1,0:T(8,128)}, f32[144,1152]{1,0:T(8,128)}, u32[]{:S(2)}, u32[]{:S(2)}) %collective-permute-start.10) | collective-permute-done | bytes 663584 | tf_op jit(solution)/shard_map/ppermute | solution.py:419
  241.4 2.0 collective-permute-done
  245.4 11.0 %collective-permute-done.14.refs_10_ = f32[144,1152]{1,0:T(8,128)S(1)} collective-permute-done((f32[144,1152]{1,0:T(8,128)}, f32[144,1152]{1,0:T(8,128)S(1)}, u32[]{:S(2)}, u32[]{:S(2)}) %collective-permute-start.14) | collective-permute-done | bytes 663584 | tf_op jit(solution)/shard_map/ppermute | solution.py:422
  267.0 18.4 %collective-permute-done.21.refs_8_ = f32[144,1152]{1,0:T(8,128)S(1)} collective-permute-done((f32[144,1152]{1,0:T(8,128)}, f32[144,1152]{1,0:T(8,128)S(1)}, u32[]{:S(2)}, u32[]{:S(2)}) %collective-permute-start.21) | collective-permute-done | bytes 663584 | tf_op jit(solution)/shard_map/ppermute | solution.py:422
  285.3 2.4 collective-permute-start.16
  288.2 25.5 %collective-permute-done.3.refs_8_ = f32[144,1152]{1,0:T(8,128)} collective-permute-done((f32[144,1152]{1,0:T(8,128)}, f32[144,1152]{1,0:T(8,128)}, u32[]{:S(2)}, u32[]{:S(2)}) %collective-permute-start.3) | collective-permute-done | bytes 663584 | tf_op jit(solution)/shard_map/ppermute | solution.py:422
  314.6 13.1 %collective-permute-done.16.refs_12_ = f32[144,1152]{1,0:T(8,128)} collective-permute-done((f32[144,1152]{1,0:T(8,128)S(1)}, f32[144,1152]{1,0:T(8,128)}, u32[]{:S(2)}, u32[]{:S(2)}) %collective-permute-start.16) | collective-permute-done | bytes 663584 | tf_op jit(solution)/shard_map/ppermute | solution.py:422
  331.9 11.8 %first.1.refs_0_.refs_1_ = bf16[2048,1152]{1,0:T(8,128)(2,1)} custom-call(f32[2048,1152]{1,0:T(8,128)} %x_ref.3, s32[2048,1]{1,0:T(8,128)} %bitcast.77, f32[4,6,8,1152]{3,2,1,0:T(8,128)} %pad.17.mod_ref.refs_13_), custom_call_target="tpu_custom_call" | custom-call | flops 47185920 | bytes 14155776 | tf_op jit(solution)/shard_map/first/pallas_call | solution.py:350
  343.8 17.3 %attend.4 = (bf16[12,72,2048]{2,1,0:T(8,128)(2,1)}, bf16[288,2048]{1,0:T(8,128)(2,1)}, f32[4,4,512]{2,1,0:T(4,128)}) custom-call(bf16[2048,1152]{1,0:T(8,128)(2,1)} %first.1.refs_0_.refs_1_, s32[2048,1]{1,0:T(8,128)} %bitcast.78, s32[4,1,512]{2,1,0:T(1,128)} %compare_select_fusion.refs_2_.refs_3_.refs_4_, f32[4,4,512]{2,1,0:T(4,128)} %get-tuple-element.193.refs_3_.refs_5_, ...), custom_call_target="tpu_custom_call" | custom-call | flops 5284823040 | bytes 14745600 | tf_op jit(solution)/shard_map/attend/pallas_call | solution.py:350
  362.3 18.4 %attend.6 = (bf16[12,72,2048]{2,1,0:T(8,128)(2,1)}, bf16[288,2048]{1,0:T(8,128)(2,1)}, f32[4,4,512]{2,1,0:T(4,128)}, bf16[1152,1152]{1,0:T(8,128)(2,1)}) custom-call(s32[1]{0:T(128)} %bitcast.6.refs_0_, bf16[2048,1152]{1,0:T(8,128)(2,1)} %first.1.refs_0_.refs_1_, s32[2048,1]{1,0:T(8,128)} %bitcast.79, ...), custom_call_target="tpu_custom_call" | custom-call | flops 5284823040 | bytes 14745600 | tf_op jit(solution)/shard_map/attend/pallas_call | solution.py:350
  381.5 18.4 %attend.7 = (bf16[12,72,2048]{2,1,0:T(8,128)(2,1)}, bf16[288,2048]{1,0:T(8,128)(2,1)}, f32[4,4,512]{2,1,0:T(4,128)}, bf16[1152,1152]{1,0:T(8,128)(2,1)}) custom-call(s32[1]{0:T(128)} %bitcast.6.refs_0_, bf16[2048,1152]{1,0:T(8,128)(2,1)} %first.1.refs_0_.refs_1_, s32[2048,1]{1,0:T(8,128)} %bitcast.80, ...), custom_call_target="tpu_custom_call" | custom-call | flops 5284823040 | bytes 14745600 | tf_op jit(solution)/shard_map/attend/pallas_call | solution.py:350
  401.4 18.5 %attend.5 = (bf16[12,72,2048]{2,1,0:T(8,128)(2,1)}, bf16[288,2048]{1,0:T(8,128)(2,1)}, f32[4,4,512]{2,1,0:T(4,128)}, bf16[1152,1152]{1,0:T(8,128)(2,1)}) custom-call(s32[1]{0:T(128)} %bitcast.6.refs_0_, bf16[2048,1152]{1,0:T(8,128)(2,1)} %first.1.refs_0_.refs_1_, s32[2048,1]{1,0:T(8,128)} %bitcast.81, ...), custom_call_target="tpu_custom_call" | custom-call | flops 5284823040 | bytes 14745600 | tf_op jit(solution)/shard_map/attend/pallas_call | solution.py:350
  419.9 34.0 %middle.1 = (f32[2048,1152]{1,0:T(8,128)}, f32[2048,1152]{1,0:T(8,128)}, bf16[2048,1152]{1,0:T(8,128)(2,1)}, bf16[2048,1152]{1,0:T(8,128)(2,1)}, f32[2048,1]{1,0:T(8,128)}, /*index=5*/f32[1,1152]{1,0:T(1,128)}) custom-call(bf16[288,2048]{1,0:T(8,128)(2,1)} %get-tuple-element.58.refs_0_.refs_2_, bf16[288,2048]{1,0:T(8,128)(2,1)} %get-tuple-element.59.refs_1_, ...), custom_call_target="tpu_custom_call" | custom-call | flops 5435817984 | bytes 51904512 | tf_op jit(solution)/shard_map/middle/pallas_call | solution.py:350
  453.9 36.9 %mlp.5 = (f32[2048,1152]{1,0:T(8,128)}, f32[2048,1152]{1,0:T(8,128)}, bf16[2048,1152]{1,0:T(8,128)(2,1)}, bf16[2048,1152]{1,0:T(8,128)(2,1)}, f32[1,1152]{1,0:T(1,128)}) custom-call(bf16[2048,1152]{1,0:T(8,128)(2,1)} %get-tuple-element.67.refs_0_, bf16[2048,1152]{1,0:T(8,128)(2,1)} %get-tuple-element.68.refs_1_, s32[2048,1]{1,0:T(8,128)} %bitcast.83, ...), custom_call_target="tpu_custom_call" | custom-call | flops 21743271936 | bytes 47185920 | tf_op jit(solution)/shard_map/mlp/pallas_call | solution.py:350
  490.8 38.3 %mlp.4 = (f32[2048,1152]{1,0:T(8,128)}, f32[2048,1152]{1,0:T(8,128)}) custom-call(bf16[2048,1152]{1,0:T(8,128)(2,1)} %get-tuple-element.67.refs_0_, bf16[2048,1152]{1,0:T(8,128)(2,1)} %get-tuple-element.68.refs_1_, s32[2048,1]{1,0:T(8,128)} %bitcast.84, f32[4,8,1152]{2,1,0:T(8,128)} %pad.19.refs_3_, f32[1,1152]{1,0:T(1,128)} %reshape.363.refs_4_, ...), custom_call_target="tpu_custom_call" | custom-call | flops 21743271936 | bytes 47185920 | tf_op jit(solution)/shard_map/mlp/pallas_call | solution.py:350
  529.1 38.9 %mlp.6 = (f32[2048,1152]{1,0:T(8,128)}, f32[2048,1152]{1,0:T(8,128)}) custom-call(bf16[2048,1152]{1,0:T(8,128)(2,1)} %get-tuple-element.67.refs_0_, bf16[2048,1152]{1,0:T(8,128)(2,1)} %get-tuple-element.68.refs_1_, s32[2048,1]{1,0:T(8,128)} %bitcast.85, f32[4,8,1152]{2,1,0:T(8,128)} %pad.20.refs_3_, ...), custom_call_target="tpu_custom_call", output_to_operand_aliasing={{0}: (6, {}), {1}: (7, {})} | custom-call | flops 21743271936 | bytes 47185920 | tf_op jit(solution)/shard_map/mlp/pallas_call | solution.py:350
  568.0 41.0 %mlp.7 = (f32[2048,1152]{1,0:T(8,128)}, f32[2048,1152]{1,0:T(8,128)}) custom-call(bf16[2048,1152]{1,0:T(8,128)(2,1)} %get-tuple-element.67.refs_0_, bf16[2048,1152]{1,0:T(8,128)(2,1)} %get-tuple-element.68.refs_1_, s32[2048,1]{1,0:T(8,128)} %bitcast.86, f32[4,8,1152]{2,1,0:T(8,128)} %pad.18.refs_3_, ...), custom_call_target="tpu_custom_call", output_to_operand_aliasing={{0}: (6, {}), {1}: (7, {})} | custom-call | flops 21743271936 | bytes 47185920 | tf_op jit(solution)/shard_map/mlp/pallas_call | solution.py:350
  609.0 41.0 %turn.1 = (f32[2048,1152]{1,0:T(8,128)}, f32[2048,1152]{1,0:T(8,128)}, bf16[2048,1152]{1,0:T(8,128)(2,1)}, f32[2048,1]{1,0:T(8,128)}, f32[4,4,8,1152]{3,2,1,0:T(8,128)}, /*index=5*/f32[1,1152]{1,0:T(1,128)}) custom-call(f32[2048,1152]{1,0:T(8,128)} %get-tuple-element.65.middle_ref, f32[2048,1152]{1,0:T(8,128)} %get-tuple-element.66.branch_ref, ...), custom_call_target="tpu_custom_call" | custom-call | flops 141557760 | bytes 70778880 | tf_op jit(solution)/shard_map/turn/pallas_call | solution.py:350
  650.0 99.9 %attend_back.1 = (f32[2048,1152]{1,0:T(8,128)}, f32[1152,1152]{1,0:T(8,128)}, f32[864,1]{1,0:T(8,128)}) custom-call(bf16[2048,1152]{1,0:T(8,128)(2,1)} %get-tuple-element.80.refs_0_, bf16[2048,1152]{1,0:T(8,128)(2,1)} %first.1.refs_0_.refs_1_, bf16[288,2048]{1,0:T(8,128)(2,1)} %get-tuple-element.58.refs_0_.refs_2_, s32[2048,1]{1,0:T(8,128)} %bitcast.88, ...), custom_call_target="tpu_custom_call" | custom-call | flops 33822867456 | bytes 47185920 | tf_op jit(solution)/shard_map/attend_back/pallas_call | solution.py:350
  749.9 20.6 %last.1 = (f32[2048,1152]{1,0:T(8,128)}, f32[4,2,8,1152]{3,2,1,0:T(8,128)}) custom-call(f32[2048,1152]{1,0:T(8,128)} %x_ref.3, f32[2048,1152]{1,0:T(8,128)} %get-tuple-element.89.fg_ref, f32[2048,1152]{1,0:T(8,128)} %get-tuple-element.90.mg_ref, s32[2048,1]{1,0:T(8,128)} %bitcast.89, f32[4,6,8,1152]{3,2,1,0:T(8,128)} %pad.17.mod_ref.refs_13_), custom_call_target="tpu_custom_call" | custom-call | flops 94371840 | bytes 37748736 | tf_op jit(solution)/shard_map/last/pallas_call | solution.py:350
  772.5 12.5 %fusion.40 = f32[1152,1152]{1,0:T(8,128)} fusion(bf16[2048,1152]{1,0:T(8,128)(2,1)} %get-tuple-element.67.refs_0_, bf16[2048,1152]{1,0:T(8,128)(2,1)} %get-tuple-element.97), kind=kOutput, calls=%fused_computation.83 | convolution fusion | flops 5435817984 | bytes 14745600 | tf_op jit(solution)/shard_map/dot_general | solution.py:57
  785.0 12.7 %fusion.41 = f32[1152,1152]{1,0:T(8,128)} fusion(bf16[2048,1152]{1,0:T(8,128)(2,1)} %get-tuple-element.99, bf16[2048,1152]{1,0:T(8,128)(2,1)} %get-tuple-element.68.refs_1_), kind=kOutput, calls=%fused_computation.84 | convolution fusion | flops 5435817984 | bytes 14745600 | tf_op jit(solution)/shard_map/dot_general | solution.py:57
  798.5 8.9 all-gather
  810.5 25.4 %all-reduce.5 = (f32[3,288]{1,0:T(4,128)S(1)}, f32[1152]{0:T(1024)}, f32[1152]{0:T(1024)}, f32[1152]{0:T(1024)}) all-reduce(f32[3,288]{1,0:T(4,128)S(1)} %reshape.374, f32[1152]{0:T(1024)S(1)} %reduce.4, f32[1152]{0:T(1024)S(1)} %reduce.5, f32[1152]{0:T(1024)S(1)} %reduce.6), channel_id=1, replica_groups=mesh['dp'=8,'mp'=4] {'dp'}, use_global_device_ids=true, to_apply=%region_5.6 | all-reduce | flops 4320 | bytes 34560 | tf_op jit(solution)/shard_map/psum | solution.py:749
  837.1 2.3 reshape.381
  839.4 3.5 fusion.6
  842.9 3.8 copy.163
  846.6 2.3 reduce_sum.22
  849.6 6.2 fusion.39
  856.9 1.8 fusion.1
  858.7 161.1 %all-reduce.12.cloned.1.call-done = (f32[1152,1152]{1,0:T(8,128)}, f32[1152,1152]{1,0:T(8,128)}, f32[1152,1152]{1,0:T(8,128)}) async-done(((f32[1152,1152]{1,0:T(8,128)}, f32[1152,1152]{1,0:T(8,128)}, f32[1152,1152]{1,0:T(8,128)}), (f32[1152,1152]{1,0:T(8,128)}, f32[1152,1152]{1,0:T(8,128)}, f32[1152,1152]{1,0:T(8,128)})) %all-reduce.12.cloned.1.call-update) | async-done | bytes 15925264 | tf_op jit(solution)/shard_map/psum | solution.py:749
  1019.7 4.5 slice.219
  1024.2 2.6 slice.222
  1026.8 2.4 copy.172
  1029.2 2.4 copy.173
  (259 shorter events, 49.1 us)
Async XLA Ops:
  8.0 321.8 %all-reduce.10.cloned.1.call-start = ((), (), s32[]{:S(2)}) async-start(), calls=%async_computation | async-start | bytes 884736 | tf_op jit(solution)/shard_map/psum | solution.py:484
  14.7 69.3 %collective-permute-start.28 = (f32[288,1152]{1,0:T(8,128)}, f32[288,1152]{1,0:T(8,128)}, u32[]{:S(2)}, u32[]{:S(2)}) collective-permute-start(f32[288,1152]{1,0:T(8,128)} %maximum_convert_fusion), channel_id=1, source_target_pairs={{0,2},{1,3},{2,0},{3,1},{4,6},{5,7},{6,4},{7,5},{8,10},{9,11},{10,... | collective-permute-start | bytes 3981320 | tf_op jit(solution)/shard_map/ppermute | solution.py:419
  24.3 130.7 %copy-start.18 = (s32[4,3,4]{2,0,1:T(4,128)S(1)}, s32[4,3,4]{2,0,1:T(4,128)}, u32[]{:S(2)}) copy-start(s32[4,3,4]{2,0,1:T(4,128)} %param.27) | copy-start | bytes 580
  24.3 130.8 %copy-start.19 = (s32[4,3,4]{2,0,1:T(4,128)S(1)}, s32[4,3,4]{2,0,1:T(4,128)}, u32[]{:S(2)}) copy-start(s32[4,3,4]{2,0,1:T(4,128)} %param.28) | copy-start | bytes 580
  24.3 130.9 %copy-start.23 = (f32[2,288]{1,0:T(2,128)S(1)}, f32[2,288]{1,0:T(2,128)}, u32[]{:S(2)}) copy-start(f32[2,288]{1,0:T(2,128)} %param.35) | copy-start | bytes 6916
  24.3 130.9 %copy-start.10 = (f32[1152]{0:T(1024)S(1)}, f32[1152]{0:T(1024)}, u32[]{:S(2)}) copy-start(f32[1152]{0:T(1024)} %param.39) | copy-start | bytes 13828
  24.3 161.6 %copy-start.1 = (bf16[3,1152,288]{1,2,0:T(8,128)(2,1)S(1)}, bf16[3,1152,288]{1,2,0:T(8,128)(2,1)}, u32[]{:S(2)}) copy-start(bf16[3,1152,288]{1,2,0:T(8,128)(2,1)} %param.34) | copy-start | bytes 5971972
  24.3 161.6 %copy-start.3 = (bf16[288,1152]{1,0:T(8,128)(2,1)S(1)}, bf16[288,1152]{1,0:T(8,128)(2,1)}, u32[]{:S(2)}) copy-start(bf16[288,1152]{1,0:T(8,128)(2,1)} %param.36) | copy-start | bytes 1990660
  28.3 162.2 %copy-start.26 = (s32[4,3]{1,0:T(4,128)S(1)}, s32[4,3]{1,0:T(4,128)}, u32[]{:S(2)}) copy-start(s32[4,3]{1,0:T(4,128)} %param.23) | copy-start | bytes 148
  28.3 162.6 %copy-start.39 = (s32[4]{0:T(128)S(1)}, s32[4]{0:T(128)}, u32[]{:S(2)}) copy-start(s32[4]{0:T(128)} %param.24) | copy-start | bytes 52
  28.3 162.7 %copy-start.15 = (s32[2048]{0:T(1024)S(1)}, s32[2048]{0:T(1024)}, u32[]{:S(2)}) copy-start(s32[2048]{0:T(1024)} %param.29) | copy-start | bytes 24580
  32.1 458.7 %all-gather.9.cloned.1.call-start = ((), (), s32[]{:S(2)}) async-start(), calls=%async_computation.2 | async-start | bytes 11943936 | tf_op jit(solution)/shard_map/all_gather | solution.py:448
  84.1 445.1 %all-gather.11.cloned.1.call-start = ((), (), s32[]{:S(2)}) async-start(), calls=%async_computation.3 | async-start | bytes 11943936 | tf_op jit(solution)/shard_map/all_gather | solution.py:448
  84.1 37.7 %collective-permute-start.29 = (f32[288,1152]{1,0:T(8,128)}, f32[288,1152]{1,0:T(8,128)}, u32[]{:S(2)}, u32[]{:S(2)}) collective-permute-start(f32[288,1152]{1,0:T(8,128)} %maximum_convert_fusion), channel_id=1, source_target_pairs={{0,1},{1,0},{2,3},{3,2},{4,5},{5,4},{6,7},{7,6},{8,9},{9,8},{10,11... | collective-permute-start | bytes 3981320 | tf_op jit(solution)/shard_map/ppermute | solution.py:419
  121.8 446.2 %all-gather.7.cloned.1.call-start = ((), (), s32[]{:S(2)}) async-start(), calls=%async_computation.1 | async-start | bytes 11943936 | tf_op jit(solution)/shard_map/all_gather | solution.py:448
  121.9 33.0 %collective-permute-start.27 = (f32[288,1152]{1,0:T(8,128)}, f32[288,1152]{1,0:T(8,128)}, u32[]{:S(2)}, u32[]{:S(2)}) collective-permute-start(f32[288,1152]{1,0:T(8,128)} %maximum_convert_fusion), channel_id=1, source_target_pairs={{0,3},{1,2},{2,1},{3,0},{4,7},{5,6},{6,5},{7,4},{8,11},{9,10},{10,... | collective-permute-start | bytes 3981320 | tf_op jit(solution)/shard_map/ppermute | solution.py:419
  154.9 682.2 %all-gather.13.cloned.1.call-start = ((), (), s32[]{:S(2)}) async-start(), calls=%async_computation.4 | async-start | bytes 3981312 | tf_op jit(solution)/shard_map/all_gather | solution.py:737
  155.3 84.4 %collective-permute-start.9 = (f32[2112]{0:T(1024)S(1)}, f32[2112]{0:T(1024)S(1)}, u32[]{:S(2)}, u32[]{:S(2)}) collective-permute-start(f32[2112]{0:T(1024)S(1)} %concatenate.30), channel_id=1, source_target_pairs={{0,2},{1,3},{2,0},{3,1},{4,6},{5,7},{6,4},{7,5},{8,10},{9,11},{10,... | collective-permute-start | bytes 25352 | tf_op jit(solution)/shard_map/ppermute | solution.py:419
  184.8 55.0 %collective-permute-start.18 = (f32[2112]{0:T(1024)S(1)}, f32[2112]{0:T(1024)S(1)}, u32[]{:S(2)}, u32[]{:S(2)}) collective-permute-start(f32[2112]{0:T(1024)S(1)} %concatenate.30), channel_id=1, source_target_pairs={{0,3},{1,2},{2,1},{3,0},{4,7},{5,6},{6,5},{7,4},{8,11},{9,10},{10,... | collective-permute-start | bytes 25352 | tf_op jit(solution)/shard_map/ppermute | solution.py:419
  187.0 44.7 %collective-permute-start.10 = (f32[144,1152]{1,0:T(8,128)}, f32[144,1152]{1,0:T(8,128)}, u32[]{:S(2)}, u32[]{:S(2)}) collective-permute-start(f32[144,1152]{1,0:T(8,128)} %fusion.3), channel_id=1, source_target_pairs={{0,2},{1,3},{2,0},{3,1},{4,6},{5,7},{6,4},{7,5},{8,10},{9,11},{10,... | collective-permute-start | bytes 1990664 | tf_op jit(solution)/shard_map/ppermute | solution.py:419
  187.0 56.4 %collective-permute-start.19 = (f32[144,1152]{1,0:T(8,128)}, f32[144,1152]{1,0:T(8,128)}, u32[]{:S(2)}, u32[]{:S(2)}) collective-permute-start(f32[144,1152]{1,0:T(8,128)} %fusion.3), channel_id=1, source_target_pairs={{0,3},{1,2},{2,1},{3,0},{4,7},{5,6},{6,5},{7,4},{8,11},{9,10},{10,... | collective-permute-start | bytes 1990664 | tf_op jit(solution)/shard_map/ppermute | solution.py:419
  189.6 55.3 %collective-permute-start.1 = (f32[144,1152]{1,0:T(8,128)}, f32[144,1152]{1,0:T(8,128)}, u32[]{:S(2)}, u32[]{:S(2)}) collective-permute-start(f32[144,1152]{1,0:T(8,128)} %fusion.3), channel_id=1, source_target_pairs={{0,1},{1,0},{2,3},{3,2},{4,5},{5,4},{6,7},{7,6},{8,9},{9,8},{10,11... | collective-permute-start | bytes 1990664 | tf_op jit(solution)/shard_map/ppermute | solution.py:419
  191.6 138.3 %copy-start.9 = (f32[6,1152]{1,0:T(8,128)S(1)}, f32[6,1152]{1,0:T(8,128)}, u32[]{:S(2)}) copy-start(f32[6,1152]{1,0:T(8,128)} %param.33) | copy-start | bytes 82948
  231.7 24.8 %collective-permute-start.14 = (f32[144,1152]{1,0:T(8,128)}, f32[144,1152]{1,0:T(8,128)S(1)}, u32[]{:S(2)}, u32[]{:S(2)}) collective-permute-start(f32[144,1152]{1,0:T(8,128)} %collective-permute-done.10.refs_6_), channel_id=1, source_target_pairs={{0,16},{4,20},{8,24},{12,28},{16,0},{20,4},{24,8},{28,12},{1,17},{... | collective-permute-start | bytes 1990664 | tf_op jit(solution)/shard_map/ppermute | solution.py:422
  239.7 3.7 collective-permute-start
  239.7 25.2 %collective-permute-start.12 = (f32[144,1152]{1,0:T(8,128)}, f32[144,1152]{1,0:T(8,128)S(1)}, u32[]{:S(2)}, u32[]{:S(2)}) collective-permute-start(f32[144,1152]{1,0:T(8,128)} %collective-permute-done.10.refs_6_), channel_id=1, source_target_pairs={{0,8},{4,12},{8,0},{12,4},{16,24},{20,28},{24,16},{28,20},{1,9},{5... | collective-permute-start | bytes 1990664 | tf_op jit(solution)/shard_map/ppermute | solution.py:422
  243.4 23.0 %collective-permute-start.11 = (f32[144,1152]{1,0:T(8,128)}, f32[144,1152]{1,0:T(8,128)}, u32[]{:S(2)}, u32[]{:S(2)}) collective-permute-start(f32[144,1152]{1,0:T(8,128)} %collective-permute-done.10.refs_6_), channel_id=1, source_target_pairs={{0,4},{4,0},{8,12},{12,8},{16,20},{20,16},{24,28},{28,24},{1,5},{5... | collective-permute-start | bytes 1990664 | tf_op jit(solution)/shard_map/ppermute | solution.py:422
  243.4 41.9 %collective-permute-start.21 = (f32[144,1152]{1,0:T(8,128)}, f32[144,1152]{1,0:T(8,128)S(1)}, u32[]{:S(2)}, u32[]{:S(2)}) collective-permute-start(f32[144,1152]{1,0:T(8,128)} %collective-permute-done.19.refs_6_), channel_id=1, source_target_pairs={{0,8},{4,12},{8,0},{12,4},{16,24},{20,28},{24,16},{28,20},{1,9},{5... | collective-permute-start | bytes 1990664 | tf_op jit(solution)/shard_map/ppermute | solution.py:422
  244.9 42.8 %collective-permute-start.23 = (f32[144,1152]{1,0:T(8,128)}, f32[144,1152]{1,0:T(8,128)}, u32[]{:S(2)}, u32[]{:S(2)}) collective-permute-start(f32[144,1152]{1,0:T(8,128)} %collective-permute-done.19.refs_6_), channel_id=1, source_target_pairs={{0,16},{4,20},{8,24},{12,28},{16,0},{20,4},{24,8},{28,12},{1,17},{... | collective-permute-start | bytes 1990664 | tf_op jit(solution)/shard_map/ppermute | solution.py:422
  256.4 87.3 %copy-start.27 = (f32[144,1152]{1,0:T(8,128)}, f32[144,1152]{1,0:T(8,128)S(1)}, u32[]{:S(2)}) copy-start(f32[144,1152]{1,0:T(8,128)S(1)} %collective-permute-done.14.refs_10_) | copy-start | bytes 1990660
  256.4 31.3 %collective-permute-start.20 = (f32[144,1152]{1,0:T(8,128)}, f32[144,1152]{1,0:T(8,128)}, u32[]{:S(2)}, u32[]{:S(2)}) collective-permute-start(f32[144,1152]{1,0:T(8,128)} %collective-permute-done.19.refs_6_), channel_id=1, source_target_pairs={{0,4},{4,0},{8,12},{12,8},{16,20},{20,16},{24,28},{28,24},{1,5},{5... | collective-permute-start | bytes 1990664 | tf_op jit(solution)/shard_map/ppermute | solution.py:422
  264.9 78.9 %copy-start.28 = (f32[144,1152]{1,0:T(8,128)}, f32[144,1152]{1,0:T(8,128)S(1)}, u32[]{:S(2)}) copy-start(f32[144,1152]{1,0:T(8,128)S(1)} %collective-permute-done.12.refs_8_) | copy-start | bytes 1990660
  264.9 48.9 %collective-permute-start.3 = (f32[144,1152]{1,0:T(8,128)}, f32[144,1152]{1,0:T(8,128)}, u32[]{:S(2)}, u32[]{:S(2)}) collective-permute-start(f32[144,1152]{1,0:T(8,128)} %collective-permute-done.1.refs_6_), channel_id=1, source_target_pairs={{0,8},{4,12},{8,0},{12,4},{16,24},{20,28},{24,16},{28,20},{1,9},{5... | collective-permute-start | bytes 1990664 | tf_op jit(solution)/shard_map/ppermute | solution.py:422
  266.4 48.2 %collective-permute-start.5 = (f32[144,1152]{1,0:T(8,128)}, f32[144,1152]{1,0:T(8,128)S(1)}, u32[]{:S(2)}, u32[]{:S(2)}) collective-permute-start(f32[144,1152]{1,0:T(8,128)} %collective-permute-done.1.refs_6_), channel_id=1, source_target_pairs={{0,16},{4,20},{8,24},{12,28},{16,0},{20,4},{24,8},{28,12},{1,17},{... | collective-permute-start | bytes 1990664 | tf_op jit(solution)/shard_map/ppermute | solution.py:422
  285.3 42.3 %collective-permute-start.16 = (f32[144,1152]{1,0:T(8,128)S(1)}, f32[144,1152]{1,0:T(8,128)}, u32[]{:S(2)}, u32[]{:S(2)}) collective-permute-start(f32[144,1152]{1,0:T(8,128)S(1)} %collective-permute-done.14.refs_10_), channel_id=1, source_target_pairs={{0,8},{4,12},{8,0},{12,4},{16,24},{20,28},{24,16},{28,20},{1,9},{5... | collective-permute-start | bytes 1990664 | tf_op jit(solution)/shard_map/ppermute | solution.py:422
  287.7 40.0 %collective-permute-start.15 = (f32[144,1152]{1,0:T(8,128)S(1)}, f32[144,1152]{1,0:T(8,128)S(1)}, u32[]{:S(2)}, u32[]{:S(2)}) collective-permute-start(f32[144,1152]{1,0:T(8,128)S(1)} %collective-permute-done.14.refs_10_), channel_id=1, source_target_pairs={{0,4},{4,0},{8,12},{12,8},{16,20},{20,16},{24,28},{28,24},{1,5},{5... | collective-permute-start | bytes 1990664 | tf_op jit(solution)/shard_map/ppermute | solution.py:422
  287.7 40.6 %collective-permute-start.13 = (f32[144,1152]{1,0:T(8,128)S(1)}, f32[144,1152]{1,0:T(8,128)S(1)}, u32[]{:S(2)}, u32[]{:S(2)}) collective-permute-start(f32[144,1152]{1,0:T(8,128)S(1)} %collective-permute-done.12.refs_8_), channel_id=1, source_target_pairs={{0,4},{4,0},{8,12},{12,8},{16,20},{20,16},{24,28},{28,24},{1,5},{5... | collective-permute-start | bytes 1990664 | tf_op jit(solution)/shard_map/ppermute | solution.py:422
  313.8 30.0 %collective-permute-start.25 = (f32[144,1152]{1,0:T(8,128)S(1)}, f32[144,1152]{1,0:T(8,128)}, u32[]{:S(2)}, u32[]{:S(2)}) collective-permute-start(f32[144,1152]{1,0:T(8,128)S(1)} %collective-permute-done.21.refs_8_), channel_id=1, source_target_pairs={{0,16},{4,20},{8,24},{12,28},{16,0},{20,4},{24,8},{28,12},{1,17},{... | collective-permute-start | bytes 1990664 | tf_op jit(solution)/shard_map/ppermute | solution.py:422
  314.5 46.6 %collective-permute-start.22 = (f32[144,1152]{1,0:T(8,128)S(1)}, f32[144,1152]{1,0:T(8,128)}, u32[]{:S(2)}, u32[]{:S(2)}) collective-permute-start(f32[144,1152]{1,0:T(8,128)S(1)} %collective-permute-done.21.refs_8_), channel_id=1, source_target_pairs={{0,4},{4,0},{8,12},{12,8},{16,20},{20,16},{24,28},{28,24},{1,5},{5... | collective-permute-start | bytes 1990664 | tf_op jit(solution)/shard_map/ppermute | solution.py:422
  327.6 34.0 %collective-permute-start.24 = (f32[144,1152]{1,0:T(8,128)}, f32[144,1152]{1,0:T(8,128)}, u32[]{:S(2)}, u32[]{:S(2)}) collective-permute-start(f32[144,1152]{1,0:T(8,128)} %collective-permute-done.23.refs_10_), channel_id=1, source_target_pairs={{0,4},{4,0},{8,12},{12,8},{16,20},{20,16},{24,28},{28,24},{1,5},{5... | collective-permute-start | bytes 1990664 | tf_op jit(solution)/shard_map/ppermute | solution.py:422
  327.7 34.1 %collective-permute-start.7 = (f32[144,1152]{1,0:T(8,128)}, f32[144,1152]{1,0:T(8,128)}, u32[]{:S(2)}, u32[]{:S(2)}) collective-permute-start(f32[144,1152]{1,0:T(8,128)} %collective-permute-done.3.refs_8_), channel_id=1, source_target_pairs={{0,16},{4,20},{8,24},{12,28},{16,0},{20,4},{24,8},{28,12},{1,17},{... | collective-permute-start | bytes 1990664 | tf_op jit(solution)/shard_map/ppermute | solution.py:422
  329.4 32.8 %collective-permute-start.17 = (f32[144,1152]{1,0:T(8,128)}, f32[144,1152]{1,0:T(8,128)}, u32[]{:S(2)}, u32[]{:S(2)}) collective-permute-start(f32[144,1152]{1,0:T(8,128)} %collective-permute-done.16.refs_12_), channel_id=1, source_target_pairs={{0,4},{4,0},{8,12},{12,8},{16,20},{20,16},{24,28},{28,24},{1,5},{5... | collective-permute-start | bytes 1990664 | tf_op jit(solution)/shard_map/ppermute | solution.py:422
  343.8 36.9 %collective-permute-start.26 = (f32[144,1152]{1,0:T(8,128)}, f32[144,1152]{1,0:T(8,128)S(1)}, u32[]{:S(2)}, u32[]{:S(2)}) collective-permute-start(f32[144,1152]{1,0:T(8,128)} %collective-permute-done.25.refs_12_), channel_id=1, source_target_pairs={{0,4},{4,0},{8,12},{12,8},{16,20},{20,16},{24,28},{28,24},{1,5},{5... | collective-permute-start | bytes 1990664 | tf_op jit(solution)/shard_map/ppermute | solution.py:422
  361.1 38.8 %collective-permute-start.2 = (f32[144,1152]{1,0:T(8,128)}, f32[144,1152]{1,0:T(8,128)S(1)}, u32[]{:S(2)}, u32[]{:S(2)}) collective-permute-start(f32[144,1152]{1,0:T(8,128)} %collective-permute-done.1.refs_6_), channel_id=1, source_target_pairs={{0,4},{4,0},{8,12},{12,8},{16,20},{20,16},{24,28},{28,24},{1,5},{5... | collective-permute-start | bytes 1990664 | tf_op jit(solution)/shard_map/ppermute | solution.py:422
  361.7 38.2 %collective-permute-start.4 = (f32[144,1152]{1,0:T(8,128)}, f32[144,1152]{1,0:T(8,128)S(1)}, u32[]{:S(2)}, u32[]{:S(2)}) collective-permute-start(f32[144,1152]{1,0:T(8,128)} %collective-permute-done.3.refs_8_), channel_id=1, source_target_pairs={{0,4},{4,0},{8,12},{12,8},{16,20},{20,16},{24,28},{28,24},{1,5},{5... | collective-permute-start | bytes 1990664 | tf_op jit(solution)/shard_map/ppermute | solution.py:422
  361.8 38.2 %collective-permute-start.6 = (f32[144,1152]{1,0:T(8,128)S(1)}, f32[144,1152]{1,0:T(8,128)S(1)}, u32[]{:S(2)}, u32[]{:S(2)}) collective-permute-start(f32[144,1152]{1,0:T(8,128)S(1)} %copy-done.31), channel_id=1, source_target_pairs={{0,4},{4,0},{8,12},{12,8},{16,20},{20,16},{24,28},{28,24},{1,5},{5... | collective-permute-start | bytes 1990664 | tf_op jit(solution)/shard_map/ppermute | solution.py:422
  362.2 37.8 %collective-permute-start.8 = (f32[144,1152]{1,0:T(8,128)}, f32[144,1152]{1,0:T(8,128)S(1)}, u32[]{:S(2)}, u32[]{:S(2)}) collective-permute-start(f32[144,1152]{1,0:T(8,128)} %collective-permute-done.7.refs_12_), channel_id=1, source_target_pairs={{0,4},{4,0},{8,12},{12,8},{16,20},{20,16},{24,28},{28,24},{1,5},{5... | collective-permute-start | bytes 1990664 | tf_op jit(solution)/shard_map/ppermute | solution.py:422
  772.5 247.3 %all-reduce.12.cloned.1.call-start = ((), (), s32[]{:S(2)}) async-start(), calls=%async_computation.5 | async-start | bytes 31850496 | tf_op jit(solution)/shard_map/psum | solution.py:749
  (32 other events, 377.9 us)
Sparse Core Ops, SparseCore 0:
  32.2 76.8 all-reduce.9
Sparse Core Ops, SparseCore 1:
  84.1 64.7 all-gather.8
  150.8 63.6 all-gather.10
  216.4 101.1 all-gather.6
  772.6 33.3 all-gather.12
  811.3 208.4 all-reduce.11
